TPU v7x, 256 devices: a whole 4x4x8 slice. The times are simulated.
256 devices in a mesh: blk: 8 (over x, core), uly: 8 (over z), tp: 4 (over y).
Axes of the slice: x: 4, y: 4, z: 8, core: 2. Of those that a mesh axis runs over, the one named last changes fastest.
Arguments:
- hidden: bfloat16 [8192, 8192], P(('blk', 'uly')), may hold values from -8 to 8
- norm_gain: bfloat16 [8192], replicated, may hold values from 0.099609375 to 1.8984375
- query_key_value_weight: bfloat16 [8192, 4, 1280], P('uly', 'tp'), may hold values from -1 to 1
- w_out: bfloat16 [4096, 8192], P('tp', 'uly'), may hold values from -0.5 to 0.5
- doc_ids: int32 [8192], replicated, may hold values from 0 to 15, never falling along the last dimension, each value on 1 to 2048 neighbouring positions
- block_order: int32 [16], replicated, may hold values from 0 to 15, each once
Outputs:
- attn_out: bfloat16 [8192, 8192], P(('blk', 'tp'), 'uly')
Inputs may be any that keep to these rules, and one draw needn't show every extreme that they name: `doc_ids`: never falls along the sequence; every document holds 1 to 2048 positions and one holds exactly 2048. Array rows c * 512 to (c + 1) * 512 - 1 hold sequence block block_order[c]; every block appears once.
All inputs are finite; a program needn't handle non-finite values.
Results may differ from a plain program's by a relative error of at most 0.029.
Values may be sent and summed in bfloat16 or wider, within the bound.
A program may use at most 64 MiB of HBM per device.

v0:
```python
import math

import jax
import jax.numpy as jnp
from jax import lax
from jax.sharding import PartitionSpec as P

QUERY_HEAD_COUNT = 32
KV_HEAD_COUNT = 4
HEAD_SIZE = 128
BLOCK = 512


THETA = 500000.0
NEG_BIG = -1e30


def rope_tables(positions):
    half_dim = HEAD_SIZE // 2
    lane_ids = jnp.arange(half_dim).astype(jnp.float32)
    base_freq = jnp.power(THETA, -2.0 * lane_ids / HEAD_SIZE)
    wavelen = 2.0 * math.pi / base_freq
    smooth = (8192.0 / wavelen - 1.0) / 3.0
    blended = (1.0 - smooth) * base_freq / 8.0 + smooth * base_freq
    scaled = jnp.where(
        wavelen > 8192.0, base_freq / 8.0, jnp.where(wavelen < 2048.0, base_freq, blended)
    )
    angles = positions.astype(jnp.float32)[:, None] * scaled[None, :]
    return (jnp.cos(angles), jnp.sin(angles))


def rotate(values, cos_table, sin_table):
    half_dim = values.shape[-1] // 2
    leading = values[..., :half_dim]
    trailing = values[..., half_dim:]
    cos_part = cos_table[:, None, :]
    sin_part = sin_table[:, None, :]
    return jnp.concatenate(
        [leading * cos_part - trailing * sin_part, trailing * cos_part + leading * sin_part],
        axis=-1,
    )


def positions_of(block_order, row_ids):
    block_ids = row_ids // BLOCK
    matches = block_ids[:, None] == jnp.arange(block_order.shape[0])[None, :]
    seq_block = jnp.sum(jnp.where(matches, block_order[None, :], 0), axis=1)
    return seq_block * BLOCK + row_ids % BLOCK


def make_attend(queries, query_pos, query_seg, doc_ids, block_order):
    head_dim = queries.shape[2]
    inv_root = 1.0 / math.sqrt(head_dim)

    def attend(running, pieces, offset):
        key_piece, value_piece = pieces
        key_count = key_piece.shape[0]
        block_size = key_count
        while block_size > 1024 and block_size % 2 == 0:
            block_size = block_size // 2
        block_total = key_count // block_size
        piece_pos = positions_of(block_order, jnp.arange(key_count))
        piece_seg = jnp.take(doc_ids, piece_pos)
        stacked = (
            key_piece.reshape(block_total, block_size, head_dim),
            value_piece.reshape(block_total, block_size, head_dim),
            piece_pos.reshape(block_total, block_size),
            piece_seg.reshape(block_total, block_size),
        )

        def one_block(softmax_state, block_data):
            key_blk, value_blk, pos_blk, seg_blk = block_data
            allowed = (pos_blk[None, :] <= query_pos[:, None]) & (
                seg_blk[None, :] == query_seg[:, None]
            )
            row_max, row_sum, weighted = softmax_state
            scores = (
                jnp.einsum("qhd,kd->hqk", queries, key_blk, preferred_element_type=jnp.float32)
                * inv_root
            )
            scores = jnp.where(allowed[None, :, :], scores, NEG_BIG)
            new_max = jnp.maximum(row_max, jnp.max(scores, axis=2))
            weights = jnp.where(allowed[None, :, :], jnp.exp(scores - new_max[:, :, None]), 0.0)
            factor = jnp.exp(row_max - new_max)
            new_sum = row_sum * factor + jnp.sum(weights, axis=2)
            product = jnp.einsum(
                "hqk,kd->hqd",
                weights.astype(jnp.bfloat16),
                value_blk,
                preferred_element_type=jnp.float32,
            )
            next_state = (new_max, new_sum, weighted * factor[:, :, None] + product)
            return (next_state, None)

        final_state, unused = lax.scan(one_block, running, stacked)
        return final_state

    return attend


def on_device(hidden, norm_gain, query_key_value_weight, w_out, doc_ids, block_order):
    group_width = QUERY_HEAD_COUNT // KV_HEAD_COUNT
    heads_here = group_width // lax.axis_size("uly")
    widened = hidden.astype(jnp.float32)
    inverse_rms = lax.rsqrt(jnp.mean(widened * widened, axis=1, keepdims=True) + 1e-05)
    rms_scaled = (widened * inverse_rms * norm_gain.astype(jnp.float32)[None, :]).astype(
        jnp.bfloat16
    )
    regrouped = lax.all_to_all(rms_scaled, "uly", split_axis=1, concat_axis=0, tiled=True)
    block_len = regrouped.shape[0]
    local_weights = query_key_value_weight.reshape(
        query_key_value_weight.shape[0], (group_width + 2) * HEAD_SIZE
    )
    partial_proj = jnp.dot(regrouped, local_weights, preferred_element_type=jnp.float32)
    query_part = partial_proj[:, : group_width * HEAD_SIZE]
    pair_part = partial_proj[:, group_width * HEAD_SIZE :]
    first_row = lax.axis_index("blk") * block_len
    query_pos = positions_of(block_order, first_row + jnp.arange(block_len))
    query_seg = jnp.take(doc_ids, query_pos)
    cos_query, sin_query = rope_tables(query_pos)
    query_sum, pair_sum = (
        lax.psum_scatter(query_part, "uly", scatter_dimension=1, tiled=True),
        lax.psum_scatter(pair_part, "uly", scatter_dimension=0, tiled=True),
    )
    key_len = pair_sum.shape[0]
    key_start = first_row + lax.axis_index("uly") * key_len
    key_pos = positions_of(block_order, key_start + jnp.arange(key_len))
    cos_key, sin_key = rope_tables(key_pos)
    queries = rotate(
        query_sum.reshape(block_len, heads_here, HEAD_SIZE), cos_query, sin_query
    ).astype(jnp.bfloat16)
    keys_local = rotate(pair_sum[:, None, :HEAD_SIZE], cos_key, sin_key)[:, 0, :].astype(
        jnp.bfloat16
    )
    values_local = pair_sum[:, HEAD_SIZE:].astype(jnp.bfloat16)
    attend = make_attend(queries, query_pos, query_seg, doc_ids, block_order)
    initial = (
        jnp.full((heads_here, block_len), NEG_BIG, jnp.float32),
        jnp.zeros((heads_here, block_len), jnp.float32),
        jnp.zeros((heads_here, block_len, HEAD_SIZE), jnp.float32),
    )
    final_state = attend(
        initial,
        (
            lax.all_gather(keys_local, ("blk", "uly"), axis=0, tiled=True),
            lax.all_gather(values_local, ("blk", "uly"), axis=0, tiled=True),
        ),
        jnp.int32(0),
    )
    row_max, row_sum, weighted = final_state
    attended = (weighted / row_sum[:, :, None]).astype(jnp.bfloat16)
    head_weights = w_out.reshape(group_width, HEAD_SIZE, w_out.shape[1])
    projected_rows = jnp.einsum(
        "hqd,hdn->qn",
        lax.all_gather(attended, "uly", axis=0, tiled=True),
        head_weights,
        preferred_element_type=jnp.float32,
    )
    return lax.psum_scatter(
        projected_rows.astype(jnp.bfloat16), "tp", scatter_dimension=0, tiled=True
    )


def solution(mesh):
    return jax.shard_map(
        on_device,
        mesh=mesh,
        in_specs=(P(("blk", "uly"), None), P(), P("uly", "tp", None), P("tp", "uly"), P(), P()),
        out_specs=P(("blk", "tp"), "uly"),
        check_vma=False,
    )
```

profile of v0, /device:TPU:8, one launch (start us, length us, event | category | flops | bytes accessed | tf_op | source)
XLA Modules:
  0.0 471.1 jit_solution(8503466636216364546)
XLA Ops:
  6.5 0.9 convert_element_type.57
  7.4 4.1 copy.14
  11.5 2.7 fusion.26
  14.2 4.6 fusion.28
  18.8 59.6 %all_to_all.19 = bf16[128,8,1024]{0,2,1:T(8,128)(2,1)} all-to-all(bf16[128,8,1024]{0,2,1:T(8,128)(2,1)S(1)} %bitcast.99), channel_id=1, replica_groups=mesh['blk'=8,'uly'=8,'tp'=4] {'uly'}, dimensions={1} | all-to-all | bytes 4194304 | tf_op jit(solution)/shard_map/all_to_all | solution.py:109
  78.3 3.9 copy.15
  82.2 4.7 fusion.29
  86.9 2.3 copy-done.2
  89.2 1.1 slice.37
  90.3 0.0 all-gather.9.cloned.1.call-start
  90.4 0.1 select_reduce_fusion.2
  90.5 34.8 %reduce-scatter.4.cloned.1.call-done = f32[128,256]{0,1:T(8,128)} async-done(((f32[1024,256]{0,1:T(8,128)}), f32[128,256]{0,1:T(8,128)}) %reduce-scatter.4.cloned.1.call-update) | async-done | bytes 131088 | tf_op jit(solution)/shard_map/reduce_scatter | solution.py:123
  125.3 0.8 slice_bitcast_fusion
  126.2 0.2 fusion.45
  126.4 0.6 pad_maximum_fusion.1
  127.0 0.0 all-gather.9.cloned.1.call-update
  127.0 0.0 all-gather.5.cloned.1.call-start
  127.1 1.5 slice.55
  128.6 0.0 reduce-scatter.6.cloned.1.call-start
  128.6 4.8 %slice.41 = f32[1024,1024]{0,1:T(8,128)} slice(f32[1024,1280]{0,1:T(8,128)} %copy-done.2), slice={[0:1024], [0:1024]} | slice | bytes 8388608 | tf_op jit(solution)/shard_map/slice | solution.py:115
  133.4 0.2 all-gather.7.cloned.1.call-start
  133.7 0.2 select_reduce_fusion
  133.9 0.1 select_reduce_fusion.1
  134.1 0.1 copy-done.1
  134.2 6.1 %gather_fusion.1 = s32[1024]{0:T(1024)S(1)} fusion(s32[8192]{0:T(1024)S(1)} %copy-done.1, s32[1024]{0:T(1024)S(1)} %broadcast_clamp_fusion.1), kind=kCustom, calls=%fused_computation.1 | custom fusion | bytes 12288 | tf_op jit(solution)/shard_map/jit(_take)/gather | solution.py:119
  140.3 0.1 compare_select_fusion
  140.4 45.5 %gather_fusion = s32[8192]{0:T(1024)S(1)} fusion(s32[8192]{0:T(1024)S(1)} %copy-done.1, s32[8192]{0:T(1024)S(1)} %broadcast_clamp_fusion), kind=kCustom, calls=%fused_computation | custom fusion | bytes 98304 | tf_op jit(solution)/shard_map/jit(_take)/gather | solution.py:63
  186.0 13.1 %all-gather.9.cloned.1.call-done = bf16[8192,1,128]{0,2,1:T(8,128)(2,1)} async-done(((bf16[128,1,128]{0,2,1:T(8,128)(2,1)}), bf16[8192,1,128]{0,2,1:T(8,128)(2,1)}) %all-gather.9.cloned.1.call-update) | async-done | bytes 2097168 | tf_op jit(solution)/shard_map/all_gather | solution.py:145
  199.1 4.1 copy.22
  203.2 69.9 %all-gather.5.cloned.1.call-done = bf16[8192,128]{0,1:T(8,128)(2,1)} async-done(((bf16[128,128]{0,1:T(8,128)(2,1)}), bf16[8192,128]{0,1:T(8,128)(2,1)}) %all-gather.5.cloned.1.call-update) | async-done | bytes 2097168 | tf_op jit(solution)/shard_map/all_gather | solution.py:146
  273.1 4.1 copy.23
  277.1 52.5 %reduce-scatter.6.cloned.1.call-done = f32[1024,128]{0,1:T(8,128)} async-done(((f32[1024,1024]{0,1:T(8,128)}), f32[1024,128]{0,1:T(8,128)}) %reduce-scatter.6.cloned.1.call-update) | async-done | bytes 524304 | tf_op jit(solution)/shard_map/reduce_scatter | solution.py:122
  329.7 2.1 fusion.36
  331.8 0.8 copy.19
  332.7 55.2 %while.15 = (s32[]{:T(128)}, f32[1,1024]{1,0:T(1,128)S(1)}, f32[1,1024]{1,0:T(1,128)S(1)}, f32[1,1024,128]{2,1,0:T(8,128)S(1)}, s32[8,1024]{1,0:T(8,128)S(1)}, /...) while((s32[]{:T(128)}, f32[1,1024]{1,0:T(1,128)S(1)}, ...), condition=%wide.region_9.10_spmd.clone, body=%wide.region_6.9_spmd.clone.sunk | while | flops 560337920 | bytes 14549149 | solution.py:95
  332.7 2.4 fusion.77
  335.1 1.6 fusion.79
  336.7 2.8 fusion.81
  339.6 2.4 fusion.77
  342.0 1.6 fusion.79
  343.7 2.8 fusion.81
  346.5 2.4 fusion.77
  348.9 1.6 fusion.79
  350.6 2.8 fusion.81
  353.4 2.4 fusion.77
  355.8 1.6 fusion.79
  357.5 2.8 fusion.81
  360.3 2.4 fusion.77
  362.7 1.6 fusion.79
  364.4 2.8 fusion.81
  367.2 2.4 fusion.77
  369.6 1.6 fusion.79
  371.3 2.8 fusion.81
  374.1 2.4 fusion.77
  376.5 1.6 fusion.79
  378.2 2.8 fusion.81
  381.0 2.4 fusion.77
  383.4 1.6 fusion.79
  385.1 2.8 fusion.81
  387.9 0.9 divide_convert_fusion
  388.9 0.0 reduce-scatter.8.cloned.1.call-start
  388.9 39.8 %all-gather.7.cloned.1.call-done = bf16[8,1024,128]{2,1,0:T(8,128)(2,1)} async-done(((bf16[1,1024,128]{2,1,0:T(8,128)(2,1)}), bf16[8,1024,128]{2,1,0:T(8,128)(2,1)}) %all-gather.7.cloned.1.call-update) | async-done | bytes 2097168 | tf_op jit(solution)/shard_map/all_gather | solution.py:155
  428.7 5.9 %bitcast_convert_fusion = bf16[1024,1024]{1,0:T(8,128)(2,1)} fusion(bf16[8,1024,128]{2,1,0:T(8,128)(2,1)} %all-gather.7.cloned.1.call-done, bf16[8,128,1024]{2,1,0:T(8,128)(2,1)} %bitcast.121), kind=kOutput, calls=%fused_computation.37 | convolution fusion | flops 2148532224 | bytes 6291456 | tf_op jit(solution)/shard_map/hqd,hdn->qn/dot_general | solution.py:153
  434.6 29.7 %reduce-scatter.8.cloned.1.call-done = bf16[256,1024]{1,0:T(8,128)(2,1)} async-done(((bf16[1024,1024]{1,0:T(8,128)(2,1)}), bf16[256,1024]{1,0:T(8,128)(2,1)}) %reduce-scatter.8.cloned.1.call-update) | async-done | bytes 524304 | tf_op jit(solution)/shard_map/reduce_scatter | solution.py:159
  (63 shorter events, 0.7 us)
Async XLA Ops:
  6.5 75.7 %copy-start = (bf16[1024,1,1280]{2,0,1:T(8,128)(2,1)S(1)}, bf16[1024,1,1280]{2,0,1:T(8,128)(2,1)}, u32[]{:S(2)}) copy-start(bf16[1024,1,1280]{2,0,1:T(8,128)(2,1)} %param.10) | copy-start | bytes 7864324
  6.5 118.8 %reduce-scatter.4.cloned.1.call-start = ((), (), s32[]{:S(2)}) async-start(), calls=%async_computation.4 | async-start | bytes 1179648 | tf_op jit(solution)/shard_map/reduce_scatter | solution.py:123
  82.2 8.2 %copy-start.3 = (s32[16]{0:T(128)S(1)}, s32[16]{0:T(128)}, u32[]{:S(2)}) copy-start(s32[16]{0:T(128)} %param.13) | copy-start | bytes 196
  86.9 2.3 copy-start.2
  90.3 108.8 %all-gather.9.cloned.1.call-start = ((), (), s32[]{:S(2)}) async-start(), calls=%async_computation.9 | async-start | bytes 2129920 | tf_op jit(solution)/shard_map/all_gather | solution.py:145
  127.0 146.0 %all-gather.5.cloned.1.call-start = ((), (), s32[]{:S(2)}) async-start(), calls=%async_computation.6 | async-start | bytes 2129920 | tf_op jit(solution)/shard_map/all_gather | solution.py:146
  128.6 201.1 %reduce-scatter.6.cloned.1.call-start = ((), (), s32[]{:S(2)}) async-start(), calls=%async_computation.5 | async-start | bytes 4718592 | tf_op jit(solution)/shard_map/reduce_scatter | solution.py:122
  133.4 0.8 copy-start.1
  133.4 295.3 %all-gather.7.cloned.1.call-start = ((), (), s32[]{:S(2)}) async-start(), calls=%async_computation.7 | async-start | bytes 2359296 | tf_op jit(solution)/shard_map/all_gather | solution.py:155
  388.9 75.4 %reduce-scatter.8.cloned.1.call-start = ((), (), s32[]{:S(2)}) async-start(), calls=%async_computation.8 | async-start | bytes 2621440 | tf_op jit(solution)/shard_map/reduce_scatter | solution.py:159
Sparse Core Ops, SparseCore 0:
  90.4 34.8 reduce-scatter.3
  127.9 71.1 all-gather.8
  201.6 71.3 all-gather.4
  275.5 54.1 reduce-scatter.5
  389.0 39.6 all-gather.6
  434.7 29.5 reduce-scatter.7
where the time goes:
time: 474 us; the launch traced here: 471 us
  waiting for transfers between devices  240 us (51%)
  local copies, waits for them, and re-layouts  79.3 us (17%)
  blocking collectives  59.6 us (13%)
  matrix products  51.9 us (11%)
  other arithmetic  25.8 us (5%)
  between operations  13.7 us (3%)
    all_gather x1, waiting for transfers between devices, on_device(): lax.all_gather(values_local, ('blk', 'uly'), axis=0, tiled=True)  69.9 us
    all_to_all x1, blocking collectives, on_device(): lax.all_to_all(rms_scaled, 'uly', split_axis=1, concat_axis=0, tiled=True)  59.6 us
    reduce_scatter x1, waiting for transfers between devices, on_device(): lax.psum_scatter(query_part, 'uly', scatter_dimension=1, tiled=True)  52.5 us
    gather x2, local copies, waits for them, and re-layouts, attend(): piece_seg = jnp.take(doc_ids, piece_pos)  45.5 us
    all_gather x1, waiting for transfers between devices, on_device(): lax.all_gather(attended, 'uly', axis=0, tiled=True)  39.8 us
    reduce_scatter x1, waiting for transfers between devices, on_device(): lax.psum_scatter(pair_part, 'uly', scatter_dimension=0, tiled=True)  34.8 us
    reduce_scatter x1, waiting for transfers between devices, on_device(): lax.psum_scatter(projected_rows.astype(jnp.bfloat16), 'tp', scatter_dimen...  29.7 us
    dot_general x8, matrix products, one_block(): jnp.einsum('hqk,kd->hqd', weights.astype(jnp.bfloat16), value_blk, prefer...  22.4 us
  transfers between devices with their start and end apart: 6, of which 6 were waited for; matrix products, arithmetic and copies ran while one was open for 14% of the time, Pallas kernels for 0%

commit v1 on v0

v1 whole, which is shorter than its diff:
```python
import math

import jax
import jax.numpy as jnp
from jax import lax
from jax.experimental import pallas as pl
from jax.experimental.pallas import tpu as pltpu
from jax.sharding import PartitionSpec as P

HEAD = 128
HEADS = 8
BLOCK = 512
THETA = 500000.0
NEG_BIG = -1e30
NZ = 8
NT = 4
ROWS = 128
SUB = ROWS // NT
FEAT = 1024
COLS = (HEADS + 2) * HEAD
HALF = COLS // 2
MESH = pl.DeviceIdType.MESH
F32 = jnp.float32
BF16 = jnp.bfloat16
FAR_FIRST = (4, 3, 5, 2, 6, 1, 7)
QSCALE = math.log2(math.e) / math.sqrt(HEAD)


def remote(src, dst, send_sem, recv_sem, device):
    return pltpu.make_async_remote_copy(
        src_ref=src,
        dst_ref=dst,
        send_sem=send_sem,
        recv_sem=recv_sem,
        device_id=device,
        device_id_type=MESH,
    )


def greet(devices):
    barrier = pltpu.get_barrier_semaphore()
    for device in devices:
        pl.semaphore_signal(barrier, inc=1, device_id=device, device_id_type=MESH)
    pl.semaphore_wait(barrier, len(devices))


def dot32(a, b):
    return jnp.dot(a, b, preferred_element_type=F32)


def proj_kernel(
    hid, w, gain, cos, sin, q_out, kv_out,
    hloc, wloc, wg, xbuf, own, far, pairs, stage, inbox,
    lsem, zs, zr, ys, yr, fs, fr, rs, rr,
):
    u = lax.axis_index("uly")
    t = lax.axis_index("tp")
    t_right, t_left = lax.rem(t + 1, NT), lax.rem(t + NT - 1, NT)
    u_right, u_left = lax.rem(u + 1, NZ), lax.rem(u + NZ - 1, NZ)
    load_w = pltpu.make_async_copy(w, wloc, lsem.at[0])
    load_h = pltpu.make_async_copy(hid, hloc, lsem.at[1])
    load_w.start()
    load_h.start()
    greet(
        [{"uly": lax.rem(u + k, NZ)} for k in range(1, NZ)]
        + [{"tp": t_right}, {"tp": t_left}]
    )
    rows = pl.ds(pl.multiple_of(t * SUB, SUB), SUB)
    over_z = []
    for i, k in enumerate(FAR_FIRST):
        v = lax.rem(u + NZ - k, NZ)
        copy = remote(
            hid.at[rows, pl.ds(pl.multiple_of(v * FEAT, FEAT), FEAT)],
            xbuf.at[i, t], zs.at[i], zr.at[i], {"uly": v},
        )
        copy.start()
        over_z.append(copy)
    load_w.wait()

    def fold(c, carry):
        r = pl.ds(pl.multiple_of(c * 128, 128), 128)
        wg[r, :] = (wloc[r, :].astype(F32) * gain[r, :]).astype(BF16)
        return carry

    lax.fori_loop(0, FEAT // 128, fold, 0)
    load_h.wait()

    def square(c, acc):
        x = hloc[:, pl.ds(pl.multiple_of(c * 128, 128), 128)].astype(F32)
        return acc + x * x

    total = lax.fori_loop(0, NZ * FEAT // 128, square, jnp.zeros((ROWS, 128), F32))
    scale = lax.rsqrt(jnp.sum(total, axis=1, keepdims=True) / (NZ * FEAT) + 1e-05)
    own[...] = dot32(hloc[:, pl.ds(pl.multiple_of(u * FEAT, FEAT), FEAT)], wg[...])

    def chunk_from(i, source, direction):
        return remote(
            xbuf.at[i, source], xbuf.at[i, source], ys.at[i, direction], yr.at[i, direction],
            {"tp": t_right if direction == 0 else t_left},
        )

    def pass_on(i):
        if i % 2 == 0:
            return remote(xbuf.at[i, t_left], xbuf.at[i, t_left], fs.at[i], fr.at[i], {"tp": t_right})
        return remote(xbuf.at[i, t_right], xbuf.at[i, t_right], fs.at[i], fr.at[i], {"tp": t_left})

    def send_sum(step, direction, piece):
        return remote(
            stage.at[direction, step, piece], inbox.at[direction, step, piece],
            rs.at[direction, step, piece], rr.at[direction, step, piece],
            {"uly": u_right if direction == 0 else u_left},
        )

    def start_sum(step, direction, piece, value):
        stage[direction, step, piece] = value.astype(BF16)
        send_sum(step, direction, piece).start()

    def cols(piece):
        return slice(piece * HALF, (piece + 1) * HALF)

    count = NZ - 1
    across = lax.rem(t + 2, NT)
    for tick in range(count + 2):
        if tick < count:
            over_z[tick].wait_recv()
            chunk_from(tick, t, 0).start()
            chunk_from(tick, t, 1).start()
        i = tick - 1
        if 0 <= i < count:
            chunk_from(i, t_left, 0).wait_recv()
            chunk_from(i, t_right, 1).wait_recv()
            pass_on(i).start()
        i = tick - 2
        if 0 <= i < count:
            remote(
                xbuf.at[i, across], xbuf.at[i, across], fs.at[i], fr.at[i], {"tp": t_right}
            ).wait_recv()
            if i == 0:
                far[...] = dot32(xbuf[0].reshape(ROWS, FEAT), wg[...])
                start_sum(0, 0, 0, far[:, cols(0)])
                start_sum(0, 1, 1, far[:, cols(1)])
            elif i % 2 == 0:
                j = i // 2
                x = xbuf[i - 1 : i + 1].reshape(2 * ROWS, FEAT)
                pairs[j - 1] = dot32(x, wg[...])
                if j == 1:
                    start_sum(1, 0, 1, pairs[0, :ROWS, cols(1)])
                    start_sum(1, 1, 0, pairs[0, ROWS:, cols(0)])

    for j in range(1, 4):
        for order in range(2):
            for direction in range(2):
                piece = order if direction == 0 else 1 - order
                if j == 1 and order == 1:
                    continue
                send_sum(j - 1, direction, piece).wait_recv()
                mine = pairs[j - 1, direction * ROWS : (direction + 1) * ROWS, cols(piece)]
                start_sum(j, direction, piece, mine + inbox[direction, j - 1, piece].astype(F32))
    for direction in range(2):
        for piece in range(2):
            send_sum(3, direction, piece).wait_recv()
    for piece in range(2):
        summed = own[:, cols(piece)]
        summed = summed + inbox[0, 3, piece].astype(F32)
        summed = summed + inbox[1, 3, piece].astype(F32)
        own[:, cols(piece)] = summed * scale
    for h in range(HEADS + 1):
        x = own[:, h * HEAD : (h + 1) * HEAD]
        x = x * cos[...] + pltpu.roll(x, HEAD // 2, 1) * sin[...]
        if h < HEADS:
            q_out[h * ROWS : (h + 1) * ROWS, :] = (x * QSCALE).astype(BF16)
        else:
            kv_out[:, :HEAD] = x.astype(BF16)
    kv_out[:, HEAD:] = own[:, (HEADS + 1) * HEAD :].astype(BF16)

    for i in range(count):
        over_z[i].wait_send()
        chunk_from(i, t, 0).wait_send()
        chunk_from(i, t, 1).wait_send()
        pass_on(i).wait_send()
    for direction in range(2):
        for step in range(4):
            for piece in range(2):
                if step > 0 or piece == direction:
                    send_sum(step, direction, piece).wait_send()


ANY = pl.BlockSpec(memory_space=pl.ANY)
VM = pl.BlockSpec(memory_space=pltpu.VMEM)
DMA = pltpu.SemaphoreType.DMA


def project(hidden, weights, gain, cos, sin):
    n = NZ - 1
    return pl.pallas_call(
        proj_kernel,
        out_shape=(
            jax.ShapeDtypeStruct((HEADS * ROWS, HEAD), BF16),
            jax.ShapeDtypeStruct((ROWS, 2 * HEAD), BF16),
        ),
        in_specs=[ANY, ANY, VM, VM, VM],
        out_specs=(VM, VM),
        scratch_shapes=[
            pltpu.VMEM((ROWS, NZ * FEAT), BF16),
            pltpu.VMEM((FEAT, COLS), BF16),
            pltpu.VMEM((FEAT, COLS), BF16),
            pltpu.VMEM((n, NT, SUB, FEAT), BF16),
            pltpu.VMEM((ROWS, COLS), F32),
            pltpu.VMEM((ROWS, COLS), F32),
            pltpu.VMEM((3, 2 * ROWS, COLS), F32),
            pltpu.VMEM((2, 4, 2, ROWS, HALF), BF16),
            pltpu.VMEM((2, 4, 2, ROWS, HALF), BF16),
            DMA((2,)),
            DMA((n,)), DMA((n,)),
            DMA((n, 2)), DMA((n, 2)),
            DMA((n,)), DMA((n,)),
            DMA((2, 4, 2)), DMA((2, 4, 2)),
        ],
        compiler_params=pltpu.CompilerParams(
            collective_id=0, has_side_effects=True, vmem_limit_bytes=40 << 20
        ),
        name="project",
    )(hidden, weights, gain, cos, sin)


Z_STEPS = (0, -1, 1, -2, 2, -3, 3, -4)


def gather_kernel(kv, out, lsem, zs, zr, xs, xr, fs, fr, ss, sr):
    b = lax.axis_index("blk")
    u = lax.axis_index("uly")
    u_right, u_left = lax.rem(u + 1, NZ), lax.rem(u + NZ - 1, NZ)
    b_right, b_left, b_across = lax.rem(b + 2, 8), lax.rem(b + 6, 8), lax.rem(b + 4, 8)
    sibling = b + 1 - 2 * lax.rem(b, 2)
    own = pltpu.make_async_copy(kv, out.at[b * NZ + u], lsem)
    own.start()
    greet([{"uly": u_right}, {"uly": u_left}, {"blk": b_right}, {"blk": b_left}, {"blk": sibling}])

    def z_of(i):
        return lax.rem(u + Z_STEPS[i] + NZ, NZ)

    def shard(owner, i):
        return out.at[owner * NZ + z_of(i)]

    def z_copy(i, src, dst):
        step = Z_STEPS[i]
        return remote(src, dst, zs.at[i], zr.at[i], {"uly": u_right if step < 0 else u_left})

    def z_send(step, src_i):
        i = Z_STEPS.index(step)
        src = kv if src_i == 0 else shard(b, src_i)
        return z_copy(i, src, shard(b, src_i))

    def x_send(i, direction):
        src = kv if i == 0 else shard(b, i)
        return remote(
            src, shard(b, i), xs.at[i, direction], xr.at[i, direction],
            {"blk": b_right if direction == 0 else b_left},
        )

    def x_wait(i, direction):
        source = b_left if direction == 0 else b_right
        return remote(
            shard(source, i), shard(source, i), xs.at[i, direction], xr.at[i, direction],
            {"blk": b_right},
        )

    def pass_on(i):
        source, target = (b_left, b_right) if i % 2 == 0 else (b_right, b_left)
        return remote(shard(source, i), shard(source, i), fs.at[i], fr.at[i], {"blk": target})

    def side(i, m):
        owner = (b, b_left, b_right, b_across)[m]
        src = kv if (i == 0 and m == 0) else shard(owner, i)
        return remote(src, shard(owner, i), ss.at[i, m], sr.at[i, m], {"blk": sibling})

    def side_wait(i, m):
        off = (0, 6, 2, 4)[m]
        owner = lax.rem(sibling + off, 8)
        return remote(shard(owner, i), shard(owner, i), ss.at[i, m], sr.at[i, m], {"blk": sibling})

    z_sends = {}

    def start_z(step, src_i):
        copy = z_send(step, src_i)
        copy.start()
        z_sends[step] = copy

    for tick in range(NZ + 2):
        i = tick
        if i < NZ:
            step = Z_STEPS[i]
            if i == 0:
                start_z(-1, 0)
                start_z(1, 0)
            else:
                z_copy(i, shard(b, i), shard(b, i)).wait_recv()
                if step < 0 and step > -4:
                    start_z(step - 1, i)
                if step > 0 and step < 3:
                    start_z(step + 1, i)
            x_send(i, 0).start()
            x_send(i, 1).start()
            side(i, 0).start()
        i = tick - 1
        if 0 <= i < NZ:
            x_wait(i, 0).wait_recv()
            x_wait(i, 1).wait_recv()
            pass_on(i).start()
            side(i, 1).start()
            side(i, 2).start()
        i = tick - 2
        if 0 <= i < NZ:
            remote(
                shard(b_across, i), shard(b_across, i), fs.at[i], fr.at[i], {"blk": b_right}
            ).wait_recv()
            side(i, 3).start()
    own.wait()
    for i in range(NZ):
        for m in range(4):
            side_wait(i, m).wait_recv()
    for copy in z_sends.values():
        copy.wait_send()
    for i in range(NZ):
        x_send(i, 0).wait_send()
        x_send(i, 1).wait_send()
        pass_on(i).wait_send()
        for m in range(4):
            side(i, m).wait_send()


def gather_kv(kv):
    return pl.pallas_call(
        gather_kernel,
        out_shape=jax.ShapeDtypeStruct((8 * NZ, ROWS, 2 * HEAD), BF16),
        in_specs=[VM],
        out_specs=VM,
        scratch_shapes=[
            DMA(()),
            DMA((NZ,)), DMA((NZ,)),
            DMA((NZ, 2)), DMA((NZ, 2)),
            DMA((NZ,)), DMA((NZ,)),
            DMA((NZ, 4)), DMA((NZ, 4)),
        ],
        compiler_params=pltpu.CompilerParams(
            collective_id=1, has_side_effects=True, vmem_limit_bytes=24 << 20
        ),
        name="gather_kv",
    )(kv)


def attend_kernel(table, q, q_start, kv, out, m_ref, l_ref, acc):
    count, q_block = table[0], table[1]
    wide = HEADS * ROWS
    m_ref[...] = jnp.full((1, wide), NEG_BIG, F32)
    l_ref[...] = jnp.zeros((1, wide), F32)
    acc[...] = jnp.zeros((HEAD, wide), F32)
    lane = lax.broadcasted_iota(jnp.int32, (128, ROWS), 1)
    row = lax.broadcasted_iota(jnp.int32, (128, ROWS), 0)
    causal = row <= lane
    starts = jnp.broadcast_to(q_start[...], (128, ROWS))

    def step(i, carry):
        k_block = q_block - i
        at = table[2 + k_block]
        k = kv[at, :, :HEAD]
        v = kv[at, :, HEAD:]
        scores = lax.dot_general(
            k, q[...], (((1,), (1,)), ((), ())), preferred_element_type=F32
        )
        allowed = (row + k_block * 128 >= starts) & (causal | (i > 0))
        bias = jnp.where(allowed, 0.0, NEG_BIG)
        scores = scores + jnp.concatenate([bias] * HEADS, axis=1)
        m_old = m_ref[...]
        m_new = jnp.maximum(m_old, jnp.max(scores, axis=0, keepdims=True))
        weights = jnp.exp2(scores - m_new)
        factor = jnp.exp2(m_old - m_new)
        m_ref[...] = m_new
        l_ref[...] = l_ref[...] * factor + jnp.sum(weights, axis=0, keepdims=True)
        mixed = lax.dot_general(
            v, weights.astype(BF16), (((0,), (0,)), ((), ())), preferred_element_type=F32
        )
        acc[...] = acc[...] * factor + mixed
        return carry

    lax.fori_loop(0, count, step, 0)
    result = acc[...] / l_ref[...]
    for h in range(HEADS):
        part = result[:, h * ROWS : (h + 1) * ROWS]
        out[:, h * HEAD : (h + 1) * HEAD] = part.T.astype(BF16)


def attend(table, q, q_start, kv):
    wide = HEADS * ROWS
    return pl.pallas_call(
        attend_kernel,
        out_shape=jax.ShapeDtypeStruct((ROWS, HEADS * HEAD), BF16),
        in_specs=[pl.BlockSpec(memory_space=pltpu.SMEM), VM, VM, VM],
        out_specs=VM,
        scratch_shapes=[
            pltpu.VMEM((1, wide), F32),
            pltpu.VMEM((1, wide), F32),
            pltpu.VMEM((HEAD, wide), F32),
        ],
        compiler_params=pltpu.CompilerParams(vmem_limit_bytes=24 << 20),
        name="attend",
    )(table, q, q_start, kv)


PIECES = 2
PROWS = ROWS // PIECES
OUTW = 1024


def out_kernel(att, w, out, wloc, abuf, far_stage, near_stage, far_box, near_box,
               lsem, zs, zr, fs, fr, ns, nr):
    u = lax.axis_index("uly")
    t = lax.axis_index("tp")
    t_right, t_left = lax.rem(t + 1, NT), lax.rem(t + NT - 1, NT)
    u_right, u_left = lax.rem(u + 1, NZ), lax.rem(u + NZ - 1, NZ)
    load_w = pltpu.make_async_copy(w, wloc, lsem.at[0])
    load_w.start()
    own_copies = []
    for p in range(PIECES):
        copy = pltpu.make_async_copy(att.at[p], abuf.at[u, p], lsem.at[1 + p])
        copy.start()
        own_copies.append(copy)
    greet([{"uly": u_right}, {"uly": u_left}, {"tp": t_right}, {"tp": t_left}])

    def z_hops(p, direction):
        return 4 if (p + direction) % 2 == 0 else 3

    def chunk(direction, h):
        return lax.rem(u + NZ + (-h if direction == 0 else h), NZ)

    def z_copy(p, direction, h, source):
        src = att.at[p] if h == 0 else abuf.at[source, p]
        return remote(
            src, abuf.at[source, p], zs.at[p, direction, h], zr.at[p, direction, h],
            {"uly": u_right if direction == 0 else u_left},
        )

    def z_send(p, direction, h):
        return z_copy(p, direction, h, chunk(direction, h))

    def z_wait(p, direction, h):
        source = chunk(direction, h + 1)
        return remote(
            abuf.at[source, p], abuf.at[source, p], zs.at[p, direction, h],
            zr.at[p, direction, h], {"uly": u_right},
        )

    def z_step(p, h):
        for direction in range(2):
            hops = z_hops(p, direction)
            if h > 0 and h <= hops:
                z_wait(p, direction, h - 1).wait_recv()
            if h < hops:
                z_send(p, direction, h).start()

    def product(p, rel):
        d = lax.rem(t + rel, NT)
        x = abuf[pl.ds(2 * d, 2), p].reshape(2 * PROWS, FEAT)
        return dot32(x, wloc[...])

    def half(side):
        return slice(side * (OUTW // 2), (side + 1) * (OUTW // 2))

    def far_send(p, side):
        return remote(
            far_stage.at[p, side], far_box.at[p, side], fs.at[p, side], fr.at[p, side],
            {"tp": t_right if side == 0 else t_left},
        )

    def near_send(p, direction, side):
        return remote(
            near_stage.at[p, direction, side], near_box.at[p, direction, side],
            ns.at[p, direction, side], nr.at[p, direction, side],
            {"tp": t_right if direction == 0 else t_left},
        )

    for p in range(PIECES):
        z_step(p, 0)
    load_w.wait()
    for copy in own_copies:
        copy.wait()
    for h in range(1, 5):
        z_step(0, h)
    for p in range(PIECES):
        more = p + 1 < PIECES
        value = product(p, 2)
        for side in range(2):
            far_stage[p, side] = value[:, half(side)].astype(BF16)
            far_send(p, side).start()
        if more:
            z_step(p + 1, 1)
        right = product(p, 1)
        near_stage[p, 0, 1] = right[:, half(1)].astype(BF16)
        near_send(p, 0, 1).start()
        left = product(p, 3)
        near_stage[p, 1, 0] = left[:, half(0)].astype(BF16)
        near_send(p, 1, 0).start()
        if more:
            z_step(p + 1, 2)
        far_send(p, 0).wait_recv()
        near_stage[p, 0, 0] = (right[:, half(0)] + far_box[p, 0].astype(F32)).astype(BF16)
        near_send(p, 0, 0).start()
        far_send(p, 1).wait_recv()
        near_stage[p, 1, 1] = (left[:, half(1)] + far_box[p, 1].astype(F32)).astype(BF16)
        near_send(p, 1, 1).start()
        if more:
            z_step(p + 1, 3)
        mine = product(p, 0)
        if more:
            z_step(p + 1, 4)
        for side in range(2):
            near_send(p, 0, side).wait_recv()
            near_send(p, 1, side).wait_recv()
            summed = mine[:, half(side)] + near_box[p, 0, side].astype(F32)
            summed = summed + near_box[p, 1, side].astype(F32)
            out[:, p, :, half(side)] = summed.reshape(2, PROWS, OUTW // 2).astype(BF16)
    for p in range(PIECES):
        for direction in range(2):
            for h in range(z_hops(p, direction)):
                z_send(p, direction, h).wait_send()
            far_send(p, direction).wait_send()
            for side in range(2):
                near_send(p, direction, side).wait_send()


def project_out(attended, w):
    half = OUTW // 2
    out = pl.pallas_call(
        out_kernel,
        out_shape=jax.ShapeDtypeStruct((2, PIECES, PROWS, OUTW), BF16),
        in_specs=[ANY, ANY],
        out_specs=VM,
        scratch_shapes=[
            pltpu.VMEM((FEAT, OUTW), BF16),
            pltpu.VMEM((NZ, PIECES, PROWS, FEAT), BF16),
            pltpu.VMEM((PIECES, 2, 2 * PROWS, half), BF16),
            pltpu.VMEM((PIECES, 2, 2, 2 * PROWS, half), BF16),
            pltpu.VMEM((PIECES, 2, 2 * PROWS, half), BF16),
            pltpu.VMEM((PIECES, 2, 2, 2 * PROWS, half), BF16),
            DMA((1 + PIECES,)),
            DMA((PIECES, 2, 4)), DMA((PIECES, 2, 4)),
            DMA((PIECES, 2)), DMA((PIECES, 2)),
            DMA((PIECES, 2, 2)), DMA((PIECES, 2, 2)),
        ],
        compiler_params=pltpu.CompilerParams(
            collective_id=2, has_side_effects=True, vmem_limit_bytes=40 << 20
        ),
        name="project_out",
    )(attended.reshape(PIECES, PROWS, FEAT), w)
    return out.reshape(2 * ROWS, OUTW)


def rope_tables(positions):
    half_dim = HEAD // 2
    lane_ids = jnp.arange(half_dim).astype(F32)
    base_freq = jnp.power(THETA, -2.0 * lane_ids / HEAD)
    wavelen = 2.0 * math.pi / base_freq
    smooth = (8192.0 / wavelen - 1.0) / 3.0
    blended = (1.0 - smooth) * base_freq / 8.0 + smooth * base_freq
    scaled = jnp.where(
        wavelen > 8192.0, base_freq / 8.0, jnp.where(wavelen < 2048.0, base_freq, blended)
    )
    angles = positions.astype(F32)[:, None] * scaled[None, :]
    cos, sin = jnp.cos(angles), jnp.sin(angles)
    return jnp.concatenate([cos, cos], axis=1), jnp.concatenate([-sin, sin], axis=1)


def place(doc_ids, block_order):
    shard = lax.axis_index("blk") * NZ + lax.axis_index("uly")
    per = BLOCK // ROWS
    seq_block = lax.dynamic_index_in_dim(block_order, shard // per, 0, keepdims=False)
    first = seq_block * BLOCK + lax.rem(shard, per) * ROWS
    numbers = jnp.arange(16, dtype=jnp.int32)
    doc_start = jnp.sum((doc_ids[None, :] < numbers[:, None]).astype(jnp.int32), axis=1)
    segment = lax.dynamic_slice_in_dim(doc_ids, first, ROWS)
    q_start = jnp.sum(
        jnp.where(segment[None, :] == numbers[:, None], doc_start[:, None], 0), axis=0
    )
    where_block = jnp.sum(
        jnp.where(block_order[None, :] == numbers[:, None], numbers[None, :], 0), axis=1
    )
    shards = (where_block[:, None] * per + jnp.arange(per, dtype=jnp.int32)[None, :]).reshape(-1)
    q_block = first // ROWS
    head = jnp.stack([q_block - q_start[0] // ROWS + 1, q_block])
    return first, q_start[None, :], jnp.concatenate([head, shards])


def on_device(hidden, norm_gain, query_key_value_weight, w_out, doc_ids, block_order):
    u = lax.axis_index("uly")
    first, q_start, table = place(doc_ids, block_order)
    cos, sin = rope_tables(first + jnp.arange(ROWS, dtype=jnp.int32))
    gain = lax.dynamic_slice_in_dim(norm_gain, u * FEAT, FEAT).astype(F32)[:, None]
    weights = query_key_value_weight.reshape(FEAT, COLS)
    q, kv = project(hidden, weights, gain, cos, sin)
    kv_all = gather_kv(kv)
    attended = attend(table, q, q_start, kv_all)
    return project_out(attended, w_out)


def solution(mesh):
    return jax.shard_map(
        on_device,
        mesh=mesh,
        in_specs=(P(("blk", "uly"), None), P(), P("uly", "tp", None), P("tp", "uly"), P(), P()),
        out_specs=P(("blk", "tp"), "uly"),
        check_vma=False,
    )
```

time: 474 us -> 155 us (0.33)
  waiting for transfers between devices: 240 us -> 0 us
  Pallas kernels: 0 us -> 143 us
  local copies, waits for them, and re-layouts: 79.3 us -> 6.44 us
  blocking collectives: 59.6 us -> 0 us
  matrix products: 51.9 us -> 0 us
  other arithmetic: 25.8 us -> 3.08 us
  between operations: 13.7 us -> 0.95 us
    pallas_call x0 -> x4, Pallas kernels: none -> 143 us  [the longest x1 60.6 us: project(): pl.pallas_call(proj_kernel, out_shape=(jax.ShapeDtypeStruct((HEADS * ROWS...]
    all_gather x3 -> x0, waiting for transfers between devices: 123 us -> none  [the longest x1 69.9 us: on_device(): lax.all_gather(values_local, ('blk', 'uly'), axis=0, tiled=True)]
    reduce_scatter x3 -> x0, waiting for transfers between devices: 117 us -> none  [the longest x1 52.5 us: on_device(): lax.psum_scatter(query_part, 'uly', scatter_dimension=1, tiled=True)]
    all_to_all x1 -> x0, blocking collectives: 59.6 us -> none  [on_device(): lax.all_to_all(rms_scaled, 'uly', split_axis=1, concat_axis=0, tiled=True)]
    dot_general x18 -> x0, matrix products: 51.9 us -> none  [the longest x8 22.4 us: one_block(): jnp.einsum('hqk,kd->hqd', weights.astype(jnp.bfloat16), value_blk, prefer...]
    gather x3 -> x0, local copies, waits for them, and re-layouts: 51.7 us -> none  [the longest x2 45.5 us: attend(): piece_seg = jnp.take(doc_ids, piece_pos)]
    reduce_sum x12 -> x3, other arithmetic: 15.9 us -> 1.8 us  [the longest x1 0.94 us: place(): jnp.sum((doc_ids[None, :] < numbers[:, None]).astype(jnp.int32), axis=1)]
    unnamed x12 -> x7, local copies, waits for them, and re-layouts: 15.4 us -> 4.13 us
  transfers between devices with their start and end apart: 6 -> 0, of which waited for: 6 -> 0; matrix products, arithmetic and copies ran while one was open for 14% -> 0% of each run, Pallas kernels for 0% -> 0%
where the time goes in v1:
time: 155 us; the launch traced here: 154 us
  Pallas kernels  143 us (92%)
  local copies, waits for them, and re-layouts  6.44 us (4%)
  other arithmetic  3.08 us (2%)
    pallas_call x1, Pallas kernels, project(): pl.pallas_call(proj_kernel, out_shape=(jax.ShapeDtypeStruct((HEADS * ROWS...  60.6 us
    pallas_call x1, Pallas kernels, project_out(): pl.pallas_call(out_kernel, out_shape=jax.ShapeDtypeStruct((2, PIECES, PRO...  48 us
    pallas_call x1, Pallas kernels, gather_kv(): pl.pallas_call(gather_kernel, out_shape=jax.ShapeDtypeStruct((8 * NZ, ROW...  32.2 us
    unnamed x7, local copies, waits for them, and re-layouts  4.13 us

profile of v1, /device:TPU:8, one launch (start us, length us, event | category | flops | bytes accessed | tf_op | source)
XLA Modules:
  0.0 153.9 jit_solution(17190131053088030622)
XLA Ops:
  0.0 1.2 dynamic_slice.10
  1.9 0.8 dynamic_slice.11
  2.7 0.9 convert_reduce_fusion
  3.6 0.1 select_reduce_fusion.1
  3.9 0.8 select_reduce_fusion
  4.7 0.7 dynamic-slice_convert_fusion
  5.4 0.1 iota_add_fusion
  5.5 0.1 add.69
  5.5 0.1 pad_add_fusion.table
  5.6 0.3 fusion
  5.9 0.1 pad_maximum_fusion
  6.1 0.2 copy.8.gain
  6.3 0.0 copy-start
  6.3 1.7 %copy-done = bf16[1024,1,1280]{2,0,1:T(8,128)(2,1)S(1)} copy-done((bf16[1024,1,1280]{2,0,1:T(8,128)(2,1)S(1)}, bf16[1024,1,1280]{2,0,1:T(8,128)(2,1)}, u32[]{:S(2)}) %copy-start) | copy-done | bytes 2621464
  8.0 0.0 copy-start.2
  8.0 1.6 %copy-done.2 = bf16[128,8192]{1,0:T(8,128)(2,1)S(1)} copy-done((bf16[128,8192]{1,0:T(8,128)(2,1)S(1)}, bf16[128,8192]{1,0:T(8,128)(2,1)}, u32[]{:S(2)}) %copy-start.2) | copy-done | bytes 2097176
  9.6 60.6 %project.1 = (bf16[1024,128]{1,0:T(8,128)(2,1)S(1)}, bf16[128,256]{1,0:T(8,128)(2,1)S(1)}) custom-call(bf16[128,8192]{1,0:T(8,128)(2,1)S(1)} %copy-done.2, bf16[1024,1280]{1,0:T(8,128)(2,1)S(1)} %bitcast.10, f32[1024,1]{1,0:T(8,128)S(1)} %copy.8.gain, f32[128,128]{1,0:T(8,128)S(1)} %get-tuple-element.12.cos, f32[128,128]{1,0:T(8,128)S(1)} %get-tuple-element.13.sin), custom_call_target="tpu_custom_call" | custom-call | tf_op jit(solution)/shard_map/project/pallas_call | solution.py:195
  70.2 32.2 %gather_kv.1.kv = bf16[64,128,256]{2,1,0:T(8,128)(2,1)S(1)} custom-call(bf16[128,256]{1,0:T(8,128)(2,1)S(1)} %get-tuple-element.8.kv), custom_call_target="tpu_custom_call" | custom-call | tf_op jit(solution)/shard_map/gather_kv/pallas_call | solution.py:333
  102.4 0.0 copy-start.1
  102.4 2.7 %attend.1 = bf16[128,1024]{1,0:T(8,128)(2,1)S(1)} custom-call(s32[66]{0:T(128)S(1)} %pad_add_fusion.table, bf16[1024,128]{1,0:T(8,128)(2,1)S(1)} %get-tuple-element.7.q, s32[1,128]{1,0:T(1,128)S(1)} %bitcast.17, bf16[64,128,256]{2,1,0:T(8,128)(2,1)S(1)} %gather_kv.1.kv), custom_call_target="tpu_custom_call" | custom-call | tf_op jit(solution)/shard_map/attend/pallas_call | solution.py:395
  105.2 0.0 copy-done.1
  105.2 48.0 %project_out.1 = bf16[2,2,64,1024]{3,2,1,0:T(8,128)(2,1)S(1)} custom-call(bf16[2,64,1024]{2,1,0:T(8,128)(2,1)S(1)} %bitcast.12, bf16[1024,1024]{1,0:T(8,128)(2,1)S(1)} %copy-done.1), custom_call_target="tpu_custom_call" | custom-call | tf_op jit(solution)/shard_map/project_out/pallas_call | solution.py:533
  153.1 0.8 copy.10
  (3 shorter events, 0.0 us)
Async XLA Ops:
  6.3 1.7 %copy-start = (bf16[1024,1,1280]{2,0,1:T(8,128)(2,1)S(1)}, bf16[1024,1,1280]{2,0,1:T(8,128)(2,1)}, u32[]{:S(2)}) copy-start(bf16[1024,1,1280]{2,0,1:T(8,128)(2,1)} %param.8) | copy-start | bytes 7864324
  8.0 1.6 %copy-start.2 = (bf16[128,8192]{1,0:T(8,128)(2,1)S(1)}, bf16[128,8192]{1,0:T(8,128)(2,1)}, u32[]{:S(2)}) copy-start(bf16[128,8192]{1,0:T(8,128)(2,1)} %hid.1) | copy-start | bytes 6291460
  102.4 2.7 %copy-start.1 = (bf16[1024,1024]{1,0:T(8,128)(2,1)S(1)}, bf16[1024,1024]{1,0:T(8,128)(2,1)}, u32[]{:S(2)}) copy-start(bf16[1024,1024]{1,0:T(8,128)(2,1)} %w.1) | copy-start | bytes 6291460

commit v2 on v1

v2 whole, which is shorter than its diff:
```python
import math

import jax
import jax.numpy as jnp
import numpy as np
from jax import lax
from jax.experimental import pallas as pl
from jax.experimental.pallas import tpu as pltpu
from jax.sharding import PartitionSpec as P

HEAD = 128
HEADS = 8
BLOCK = 512
THETA = 500000.0
NEG_BIG = -1e30
NZ = 8
NT = 4
ROWS = 128
SUB = ROWS // NT
FEAT = 1024
COLS = (HEADS + 2) * HEAD
MESH = pl.DeviceIdType.MESH
F32 = jnp.float32
BF16 = jnp.bfloat16
FAR_FIRST = (4, 3, 5, 2, 6, 1, 7)
QSCALE = math.log2(math.e) / math.sqrt(HEAD)


def remote(src, dst, send_sem, recv_sem, device):
    return pltpu.make_async_remote_copy(
        src_ref=src,
        dst_ref=dst,
        send_sem=send_sem,
        recv_sem=recv_sem,
        device_id=device,
        device_id_type=MESH,
    )


def greet(devices):
    barrier = pltpu.get_barrier_semaphore()
    for device in devices:
        pl.semaphore_signal(barrier, inc=1, device_id=device, device_id_type=MESH)
    pl.semaphore_wait(barrier, len(devices))


def dot32(a, b):
    return jnp.dot(a, b, preferred_element_type=F32)


KCOL = HEADS * HEAD
PIECE_COLS = (slice(KCOL, KCOL + HEAD), slice(KCOL + HEAD, COLS), slice(0, KCOL // 2), slice(KCOL // 2, KCOL))
QUARTERED = 5
Z_STEPS = (0, -1, 1, -2, 2, -3, 3, -4)


def proj_kernel(
    order, freq, gain, hid, w, q_out, kv_all,
    hloc, wloc, wg, g32, xbuf, own, far, pairs, kv, rope,
    kv_stage, kv_inbox, q_stage, q_inbox,
    lsem, zs, zr, ys, yr, fs, fr, ks, kr, qs, qr,
    gzs, gzr, gxs, gxr, gfs, gfr, gss, gsr,
):
    b = lax.axis_index("blk")
    u = lax.axis_index("uly")
    t = lax.axis_index("tp")
    t_right, t_left, across = lax.rem(t + 1, NT), lax.rem(t + 3, NT), lax.rem(t + 2, NT)
    u_right, u_left = lax.rem(u + 1, NZ), lax.rem(u + NZ - 1, NZ)
    b_right, b_left, b_across = lax.rem(b + 2, 8), lax.rem(b + 6, 8), lax.rem(b + 4, 8)
    sibling = b + 1 - 2 * lax.rem(b, 2)
    load_w = pltpu.make_async_copy(w, wloc, lsem.at[0])
    load_h = pltpu.make_async_copy(hid, hloc, lsem.at[1])
    load_w.start()
    load_h.start()
    greet(
        [{"uly": lax.rem(u + k, NZ)} for k in range(1, NZ)]
        + [{"tp": t_right}, {"tp": t_left}, {"blk": b_right}, {"blk": b_left}, {"blk": sibling}]
    )

    def part(owner):
        return pl.ds(pl.multiple_of(owner * SUB, SUB), SUB)

    def feats(owner):
        return pl.ds(pl.multiple_of(owner * FEAT, FEAT), FEAT)

    over_z = []
    for i, k in enumerate(FAR_FIRST):
        v = lax.rem(u + NZ - k, NZ)
        if i < QUARTERED:
            src, dst = hid.at[part(t), feats(v)], xbuf.at[i, part(t)]
        else:
            src, dst = hid.at[:, feats(v)], xbuf.at[i]
        copy = remote(src, dst, zs.at[i], zr.at[i], {"uly": v})
        copy.start()
        over_z.append(copy)

    g32[...] = gain[...].astype(F32)
    load_w.wait()

    def fold(c, carry):
        r = pl.ds(pl.multiple_of(c * 128, 128), 128)
        column = jnp.broadcast_to(g32[pl.ds(u * NZ + c, 1), :], (128, 128)).T
        for n in range(COLS // 128):
            lanes = slice(n * 128, (n + 1) * 128)
            wg[r, lanes] = (wloc[r, lanes].astype(F32) * column).astype(BF16)
        return carry

    lax.fori_loop(0, FEAT // 128, fold, 0)
    load_h.wait()

    def square(c, acc):
        x = hloc[:, pl.ds(pl.multiple_of(c * 128, 128), 128)].astype(F32)
        return acc + x * x

    def chunk_from(i, source, direction):
        return remote(
            xbuf.at[i, part(source)], xbuf.at[i, part(source)],
            ys.at[i, direction], yr.at[i, direction],
            {"tp": t_right if direction == 0 else t_left},
        )

    def pass_on(i):
        source, target = (t_left, t_right) if i % 2 == 0 else (t_right, t_left)
        return remote(
            xbuf.at[i, part(source)], xbuf.at[i, part(source)], fs.at[i], fr.at[i], {"tp": target}
        )

    def kv_copy(step, direction, piece):
        return remote(
            kv_stage.at[direction, step, piece], kv_inbox.at[direction, step, piece],
            ks.at[direction, step, piece], kr.at[direction, step, piece],
            {"uly": u_right if direction == 0 else u_left},
        )

    def q_copy(step, direction, piece):
        return remote(
            q_stage.at[direction, step, piece], q_inbox.at[direction, step, piece],
            qs.at[direction, step, piece], qr.at[direction, step, piece],
            {"uly": u_right if direction == 0 else u_left},
        )

    def mine(step, direction, cols):
        if step == 0:
            return far[:, cols]
        return pairs[step - 1, direction * ROWS : (direction + 1) * ROWS, cols]

    def send_kv(step, direction, piece):
        value = mine(step, direction, PIECE_COLS[piece])
        if step > 1 or (step == 1 and piece == direction):
            kv_copy(step - 1, direction, piece).wait_recv()
            value = value + kv_inbox[direction, step - 1, piece].astype(F32)
        kv_stage[direction, step, piece] = value.astype(BF16)
        kv_copy(step, direction, piece).start()

    def send_q(step, direction, piece):
        value = mine(step, direction, PIECE_COLS[2 + piece])
        if step > 1 or (step == 1 and piece == direction):
            q_copy(step - 1, direction, piece).wait_recv()
            value = value + q_inbox[direction, step - 1, piece].astype(F32)
        q_stage[direction, step, piece] = value.astype(BF16)
        q_copy(step, direction, piece).start()

    def far_product():
        far[...] = dot32(xbuf[0], wg[...])
        for direction in range(2):
            send_kv(0, direction, direction)
        for direction in range(2):
            send_q(0, direction, direction)

    def pair_product(j):
        x = xbuf[2 * j - 1 : 2 * j + 1].reshape(2 * ROWS, FEAT)
        pairs[j - 1] = dot32(x, wg[...])

    for tick in range(QUARTERED + 2):
        if tick < QUARTERED:
            over_z[tick].wait_recv()
            chunk_from(tick, t, 0).start()
            chunk_from(tick, t, 1).start()
        i = tick - 1
        if 0 <= i < QUARTERED:
            chunk_from(i, t_left, 0).wait_recv()
            chunk_from(i, t_right, 1).wait_recv()
            pass_on(i).start()
        i = tick - 2
        if 0 <= i < QUARTERED:
            remote(
                xbuf.at[i, part(across)], xbuf.at[i, part(across)], fs.at[i], fr.at[i],
                {"tp": t_right},
            ).wait_recv()
            if i == 0:
                far_product()
            elif i % 2 == 0:
                pair_product(i // 2)
            if i == 2:
                for direction in range(2):
                    send_kv(1, direction, 1 - direction)
                    send_kv(1, direction, direction)
                for direction in range(2):
                    send_q(1, direction, 1 - direction)
    for direction in range(2):
        for piece in range(2):
            send_kv(2, direction, piece)
    for direction in range(2):
        send_q(1, direction, direction)
    over_z[QUARTERED].wait_recv()
    over_z[QUARTERED + 1].wait_recv()
    pair_product(3)
    for direction in range(2):
        for piece in range(2):
            send_kv(3, direction, piece)

    total = lax.fori_loop(0, NZ * FEAT // 128, square, jnp.zeros((ROWS, 128), F32))
    scale = lax.rsqrt(jnp.sum(total, axis=1, keepdims=True) / (NZ * FEAT) + 1e-05)
    own[...] = dot32(hloc[:, feats(u)], wg[...])
    shard_id = b * NZ + u
    block = shard_id // (BLOCK // ROWS)
    first = order[block] * BLOCK + lax.rem(shard_id, BLOCK // ROWS) * ROWS
    position = (lax.broadcasted_iota(jnp.int32, (ROWS, HEAD), 0) + first).astype(F32)
    angles = position * freq[...]
    left_half = lax.broadcasted_iota(jnp.int32, (ROWS, HEAD), 1) < HEAD // 2
    sines = jnp.sin(angles)
    rope[0] = jnp.cos(angles)
    rope[1] = jnp.where(left_half, -sines, sines)

    def rotated(x):
        return x * rope[0] + pltpu.roll(x, HEAD // 2, 1) * rope[1]

    for piece in range(2):
        kv_copy(3, 0, piece).wait_recv()
        kv_copy(3, 1, piece).wait_recv()
        x = own[:, PIECE_COLS[piece]]
        x = x + kv_inbox[0, 3, piece].astype(F32)
        x = (x + kv_inbox[1, 3, piece].astype(F32)) * scale
        if piece == 0:
            x = rotated(x)
        kv[:, piece * HEAD : (piece + 1) * HEAD] = x.astype(BF16)

    def z_of(i):
        return lax.rem(u + Z_STEPS[i] + NZ, NZ)

    def shard(owner, i):
        return kv_all.at[owner * NZ + z_of(i)]

    def held(i):
        return kv if i == 0 else shard(b, i)

    def z_copy(i, src, dst):
        to = u_right if Z_STEPS[i] < 0 else u_left
        return remote(src, dst, gzs.at[i], gzr.at[i], {"uly": to})

    def x_send(i, direction):
        return remote(
            held(i), shard(b, i), gxs.at[i, direction], gxr.at[i, direction],
            {"blk": b_right if direction == 0 else b_left},
        )

    def x_wait(i, direction):
        source = b_left if direction == 0 else b_right
        return remote(
            shard(source, i), shard(source, i), gxs.at[i, direction], gxr.at[i, direction],
            {"blk": b_right},
        )

    def x_pass(i):
        source, target = (b_left, b_right) if i % 2 == 0 else (b_right, b_left)
        return remote(shard(source, i), shard(source, i), gfs.at[i], gfr.at[i], {"blk": target})

    def side(i, m):
        owner = (b, b_left, b_right, b_across)[m]
        src = held(i) if m == 0 else shard(owner, i)
        return remote(src, shard(owner, i), gss.at[i, m], gsr.at[i, m], {"blk": sibling})

    def side_wait(i, m):
        owner = lax.rem(sibling + (0, 6, 2, 4)[m], 8)
        return remote(shard(owner, i), shard(owner, i), gss.at[i, m], gsr.at[i, m], {"blk": sibling})

    z_sends = []

    def start_z(step, src_i):
        copy = z_copy(Z_STEPS.index(step), held(src_i), shard(b, src_i))
        copy.start()
        z_sends.append(copy)

    place_own = pltpu.make_async_copy(kv, kv_all.at[b * NZ + u], lsem.at[2])

    def gather_tick(tick):
        i = tick
        if i < NZ:
            step = Z_STEPS[i]
            if i == 0:
                start_z(-1, 0)
                start_z(1, 0)
                place_own.start()
            else:
                z_copy(i, shard(b, i), shard(b, i)).wait_recv()
                if -4 < step < 0:
                    start_z(step - 1, i)
                if 0 < step < 3:
                    start_z(step + 1, i)
            x_send(i, 0).start()
            x_send(i, 1).start()
            side(i, 0).start()
        i = tick - 1
        if 0 <= i < NZ:
            x_wait(i, 0).wait_recv()
            x_wait(i, 1).wait_recv()
            x_pass(i).start()
            side(i, 1).start()
            side(i, 2).start()
        i = tick - 2
        if 0 <= i < NZ:
            remote(
                shard(b_across, i), shard(b_across, i), gfs.at[i], gfr.at[i], {"blk": b_right}
            ).wait_recv()
            side(i, 3).start()

    def finish_q(piece):
        q_copy(3, 0, piece).wait_recv()
        q_copy(3, 1, piece).wait_recv()
        cols = PIECE_COLS[2 + piece]
        x = own[:, cols] + q_inbox[0, 3, piece].astype(F32)
        own[:, cols] = (x + q_inbox[1, 3, piece].astype(F32)) * (scale * QSCALE)
        for h in range(piece * HEADS // 2, (piece + 1) * HEADS // 2):
            x = rotated(own[:, h * HEAD : (h + 1) * HEAD])
            q_out[h * ROWS : (h + 1) * ROWS, :] = x.astype(BF16)

    gather_tick(0)
    for direction in range(2):
        send_q(2, direction, direction)
    gather_tick(1)
    for direction in range(2):
        send_q(2, direction, 1 - direction)
    gather_tick(2)
    gather_tick(3)
    for direction in range(2):
        send_q(3, direction, direction)
    gather_tick(4)
    for direction in range(2):
        send_q(3, direction, 1 - direction)
    gather_tick(5)
    gather_tick(6)
    finish_q(0)
    gather_tick(7)
    finish_q(1)
    gather_tick(8)
    gather_tick(9)
    place_own.wait()
    for i in range(NZ):
        for m in range(4):
            side_wait(i, m).wait_recv()

    for copy in over_z:
        copy.wait_send()
    for i in range(QUARTERED):
        chunk_from(i, t, 0).wait_send()
        chunk_from(i, t, 1).wait_send()
        pass_on(i).wait_send()
    for direction in range(2):
        for step in range(4):
            for piece in range(2):
                if step > 0 or piece == direction:
                    kv_copy(step, direction, piece).wait_send()
                    q_copy(step, direction, piece).wait_send()
    for copy in z_sends:
        copy.wait_send()
    for i in range(NZ):
        x_send(i, 0).wait_send()
        x_send(i, 1).wait_send()
        x_pass(i).wait_send()
        for m in range(4):
            side(i, m).wait_send()


ANY = pl.BlockSpec(memory_space=pl.ANY)
VM = pl.BlockSpec(memory_space=pltpu.VMEM)
DMA = pltpu.SemaphoreType.DMA


HBM = pl.BlockSpec(memory_space=pltpu.HBM)
SM = pl.BlockSpec(memory_space=pltpu.SMEM)


def project(order, freq, gain, hidden, weights):
    n = NZ - 1
    return pl.pallas_call(
        proj_kernel,
        out_shape=(
            jax.ShapeDtypeStruct((HEADS * ROWS, HEAD), BF16),
            jax.ShapeDtypeStruct((8 * NZ, ROWS, 2 * HEAD), BF16),
        ),
        in_specs=[SM, VM, VM, HBM, HBM],
        out_specs=(VM, VM),
        scratch_shapes=[
            pltpu.VMEM((ROWS, NZ * FEAT), BF16),
            pltpu.VMEM((FEAT, COLS), BF16),
            pltpu.VMEM((FEAT, COLS), BF16),
            pltpu.VMEM((NZ * FEAT // 128, 128), F32),
            pltpu.VMEM((n, ROWS, FEAT), BF16),
            pltpu.VMEM((ROWS, COLS), F32),
            pltpu.VMEM((ROWS, COLS), F32),
            pltpu.VMEM((3, 2 * ROWS, COLS), F32),
            pltpu.VMEM((ROWS, 2 * HEAD), BF16),
            pltpu.VMEM((2, ROWS, HEAD), F32),
            pltpu.VMEM((2, 4, 2, ROWS, HEAD), BF16),
            pltpu.VMEM((2, 4, 2, ROWS, HEAD), BF16),
            pltpu.VMEM((2, 4, 2, ROWS, KCOL // 2), BF16),
            pltpu.VMEM((2, 4, 2, ROWS, KCOL // 2), BF16),
            DMA((3,)),
            DMA((n,)), DMA((n,)),
            DMA((n, 2)), DMA((n, 2)),
            DMA((n,)), DMA((n,)),
            DMA((2, 4, 2)), DMA((2, 4, 2)),
            DMA((2, 4, 2)), DMA((2, 4, 2)),
            DMA((NZ,)), DMA((NZ,)),
            DMA((NZ, 2)), DMA((NZ, 2)),
            DMA((NZ,)), DMA((NZ,)),
            DMA((NZ, 4)), DMA((NZ, 4)),
        ],
        compiler_params=pltpu.CompilerParams(
            collective_id=0, has_side_effects=True, vmem_limit_bytes=62 << 20
        ),
        name="project",
    )(order, freq, gain, hidden, weights)


def attend_kernel(order, docs, q, kv, out, inverse, m_ref, l_ref, acc):
    per = BLOCK // ROWS
    shard = lax.axis_index("blk") * NZ + lax.axis_index("uly")
    q_block = order[shard // per] * per + lax.rem(shard, per)
    for r in range(16):
        inverse[order[r]] = r
    segment = docs[pl.ds(q_block, 1), :]
    starts = jnp.zeros((1, ROWS), jnp.int32)
    for n in range(1, 16):
        before = jnp.sum((docs[...] < n).astype(jnp.int32))
        starts = jnp.where(segment == n, before, starts)
    count = q_block - jnp.min(starts) // ROWS + 1
    wide = HEADS * ROWS
    m_ref[...] = jnp.full((1, wide), NEG_BIG, F32)
    l_ref[...] = jnp.zeros((1, wide), F32)
    acc[...] = jnp.zeros((HEAD, wide), F32)
    lane = lax.broadcasted_iota(jnp.int32, (128, ROWS), 1)
    row = lax.broadcasted_iota(jnp.int32, (128, ROWS), 0)
    causal = row <= lane
    starts = jnp.broadcast_to(starts, (128, ROWS))

    def step(i, carry):
        k_block = q_block - i
        at = inverse[k_block // per] * per + lax.rem(k_block, per)
        k = kv[at, :, :HEAD]
        v = kv[at, :, HEAD:]
        scores = lax.dot_general(
            k, q[...], (((1,), (1,)), ((), ())), preferred_element_type=F32
        )
        allowed = (row + k_block * 128 >= starts) & (causal | (i > 0))
        bias = jnp.where(allowed, 0.0, NEG_BIG)
        scores = scores + jnp.concatenate([bias] * HEADS, axis=1)
        m_old = m_ref[...]
        m_new = jnp.maximum(m_old, jnp.max(scores, axis=0, keepdims=True))
        weights = jnp.exp2(scores - m_new)
        factor = jnp.exp2(m_old - m_new)
        m_ref[...] = m_new
        l_ref[...] = l_ref[...] * factor + jnp.sum(weights, axis=0, keepdims=True)
        mixed = lax.dot_general(
            v, weights.astype(BF16), (((0,), (0,)), ((), ())), preferred_element_type=F32
        )
        acc[...] = acc[...] * factor + mixed
        return carry

    lax.fori_loop(0, count, step, 0)
    result = acc[...] / l_ref[...]
    for h in range(HEADS):
        part = result[:, h * ROWS : (h + 1) * ROWS]
        out[:, h * HEAD : (h + 1) * HEAD] = part.T.astype(BF16)


def attend(order, docs, q, kv):
    wide = HEADS * ROWS
    return pl.pallas_call(
        attend_kernel,
        out_shape=jax.ShapeDtypeStruct((ROWS, HEADS * HEAD), BF16),
        in_specs=[SM, VM, VM, VM],
        out_specs=VM,
        scratch_shapes=[
            pltpu.SMEM((16,), jnp.int32),
            pltpu.VMEM((1, wide), F32),
            pltpu.VMEM((1, wide), F32),
            pltpu.VMEM((HEAD, wide), F32),
        ],
        compiler_params=pltpu.CompilerParams(vmem_limit_bytes=60 << 20),
        name="attend",
    )(order, docs, q, kv)


PIECES = 2
PROWS = ROWS // PIECES
OUTW = 1024


def out_kernel(att, w, out, wloc, abuf, far_stage, near_stage, far_box, near_box,
               lsem, zs, zr, fs, fr, ns, nr):
    u = lax.axis_index("uly")
    t = lax.axis_index("tp")
    t_right, t_left = lax.rem(t + 1, NT), lax.rem(t + NT - 1, NT)
    u_right, u_left = lax.rem(u + 1, NZ), lax.rem(u + NZ - 1, NZ)
    load_w = pltpu.make_async_copy(w, wloc, lsem.at[0])
    load_w.start()
    own_copies = []
    for p in range(PIECES):
        copy = pltpu.make_async_copy(att.at[p], abuf.at[u, p], lsem.at[1 + p])
        copy.start()
        own_copies.append(copy)
    greet([{"uly": u_right}, {"uly": u_left}, {"tp": t_right}, {"tp": t_left}])

    def z_hops(p, direction):
        return 4 if (p + direction) % 2 == 0 else 3

    def chunk(direction, h):
        return lax.rem(u + NZ + (-h if direction == 0 else h), NZ)

    def z_copy(p, direction, h, source):
        src = att.at[p] if h == 0 else abuf.at[source, p]
        return remote(
            src, abuf.at[source, p], zs.at[p, direction, h], zr.at[p, direction, h],
            {"uly": u_right if direction == 0 else u_left},
        )

    def z_send(p, direction, h):
        return z_copy(p, direction, h, chunk(direction, h))

    def z_wait(p, direction, h):
        source = chunk(direction, h + 1)
        return remote(
            abuf.at[source, p], abuf.at[source, p], zs.at[p, direction, h],
            zr.at[p, direction, h], {"uly": u_right},
        )

    def z_step(p, h):
        for direction in range(2):
            hops = z_hops(p, direction)
            if h > 0 and h <= hops:
                z_wait(p, direction, h - 1).wait_recv()
            if h < hops:
                z_send(p, direction, h).start()

    def product(p, rel):
        d = lax.rem(t + rel, NT)
        x = abuf[pl.ds(2 * d, 2), p].reshape(2 * PROWS, FEAT)
        return dot32(x, wloc[...])

    def half(side):
        return slice(side * (OUTW // 2), (side + 1) * (OUTW // 2))

    def far_send(p, side):
        return remote(
            far_stage.at[p, side], far_box.at[p, side], fs.at[p, side], fr.at[p, side],
            {"tp": t_right if side == 0 else t_left},
        )

    def near_send(p, direction, side):
        return remote(
            near_stage.at[p, direction, side], near_box.at[p, direction, side],
            ns.at[p, direction, side], nr.at[p, direction, side],
            {"tp": t_right if direction == 0 else t_left},
        )

    for p in range(PIECES):
        z_step(p, 0)
    load_w.wait()
    for copy in own_copies:
        copy.wait()
    for h in range(1, 5):
        z_step(0, h)
    for p in range(PIECES):
        more = p + 1 < PIECES
        value = product(p, 2)
        for side in range(2):
            far_stage[p, side] = value[:, half(side)].astype(BF16)
            far_send(p, side).start()
        if more:
            z_step(p + 1, 1)
        right = product(p, 1)
        near_stage[p, 0, 1] = right[:, half(1)].astype(BF16)
        near_send(p, 0, 1).start()
        left = product(p, 3)
        near_stage[p, 1, 0] = left[:, half(0)].astype(BF16)
        near_send(p, 1, 0).start()
        if more:
            z_step(p + 1, 2)
        far_send(p, 0).wait_recv()
        near_stage[p, 0, 0] = (right[:, half(0)] + far_box[p, 0].astype(F32)).astype(BF16)
        near_send(p, 0, 0).start()
        far_send(p, 1).wait_recv()
        near_stage[p, 1, 1] = (left[:, half(1)] + far_box[p, 1].astype(F32)).astype(BF16)
        near_send(p, 1, 1).start()
        if more:
            z_step(p + 1, 3)
        mine = product(p, 0)
        if more:
            z_step(p + 1, 4)
        for side in range(2):
            near_send(p, 0, side).wait_recv()
            near_send(p, 1, side).wait_recv()
            summed = mine[:, half(side)] + near_box[p, 0, side].astype(F32)
            summed = summed + near_box[p, 1, side].astype(F32)
            out[:, p, :, half(side)] = summed.reshape(2, PROWS, OUTW // 2).astype(BF16)
    for p in range(PIECES):
        for direction in range(2):
            for h in range(z_hops(p, direction)):
                z_send(p, direction, h).wait_send()
            far_send(p, direction).wait_send()
            for side in range(2):
                near_send(p, direction, side).wait_send()


def project_out(attended, w):
    half = OUTW // 2
    out = pl.pallas_call(
        out_kernel,
        out_shape=jax.ShapeDtypeStruct((2, PIECES, PROWS, OUTW), BF16),
        in_specs=[ANY, HBM],
        out_specs=VM,
        scratch_shapes=[
            pltpu.VMEM((FEAT, OUTW), BF16),
            pltpu.VMEM((NZ, PIECES, PROWS, FEAT), BF16),
            pltpu.VMEM((PIECES, 2, 2 * PROWS, half), BF16),
            pltpu.VMEM((PIECES, 2, 2, 2 * PROWS, half), BF16),
            pltpu.VMEM((PIECES, 2, 2 * PROWS, half), BF16),
            pltpu.VMEM((PIECES, 2, 2, 2 * PROWS, half), BF16),
            DMA((1 + PIECES,)),
            DMA((PIECES, 2, 4)), DMA((PIECES, 2, 4)),
            DMA((PIECES, 2)), DMA((PIECES, 2)),
            DMA((PIECES, 2, 2)), DMA((PIECES, 2, 2)),
        ],
        compiler_params=pltpu.CompilerParams(
            collective_id=2, has_side_effects=True, vmem_limit_bytes=62 << 20
        ),
        name="project_out",
    )(attended.reshape(PIECES, PROWS, FEAT), w)
    return out.reshape(2 * ROWS, OUTW)


def rope_frequencies():
    base = THETA ** (-2.0 * np.arange(HEAD // 2, dtype=np.float64) / HEAD)
    wavelen = 2.0 * np.pi / base
    smooth = (8192.0 / wavelen - 1.0) / 3.0
    blended = (1.0 - smooth) * base / 8.0 + smooth * base
    scaled = np.where(wavelen > 8192.0, base / 8.0, np.where(wavelen < 2048.0, base, blended))
    return jnp.asarray(np.tile(scaled, 2)[None, :], F32)


def on_device(hidden, norm_gain, query_key_value_weight, w_out, doc_ids, block_order):
    weights = query_key_value_weight.reshape(FEAT, COLS)
    gain = norm_gain.reshape(NZ * FEAT // 128, 128)
    docs = doc_ids.reshape(NZ * FEAT // 128, 128)
    q, kv_all = project(block_order, rope_frequencies(), gain, hidden, weights)
    attended = attend(block_order, docs, q, kv_all)
    return project_out(attended, w_out)


def solution(mesh):
    return jax.shard_map(
        on_device,
        mesh=mesh,
        in_specs=(P(("blk", "uly"), None), P(), P("uly", "tp", None), P("tp", "uly"), P(), P()),
        out_specs=P(("blk", "tp"), "uly"),
        check_vma=False,
    )
```

time: 155 us -> 136 us (0.88)
  the two profiles are of different devices: /device:TPU:8 before, /device:TPU:2 now
where the time goes in v2:
time: 136 us
  Pallas kernels  134 us (99%)
  local copies, waits for them, and re-layouts  1.87 us (1%)
    pallas_call x1, Pallas kernels, project(): pl.pallas_call(proj_kernel, out_shape=(jax.ShapeDtypeStruct((HEADS * ROWS...  78.3 us
    pallas_call x1, Pallas kernels, project_out(): pl.pallas_call(out_kernel, out_shape=jax.ShapeDtypeStruct((2, PIECES, PRO...  49.3 us
    pallas_call x1, Pallas kernels, attend(): pl.pallas_call(attend_kernel, out_shape=jax.ShapeDtypeStruct((ROWS, HEADS...  6.04 us

profile of v2, /device:TPU:2, one launch (start us, length us, event | category | flops | bytes accessed | tf_op | source)
XLA Modules:
  0.0 135.5 jit_solution(4054718760016120230)
XLA Ops:
  0.0 78.3 %project.1 = (bf16[1024,128]{1,0:T(8,128)(2,1)}, bf16[64,128,256]{2,1,0:T(8,128)(2,1)}) custom-call(s32[16]{0:T(128)} %order.3, f32[1,128]{1,0:T(1,128)} %constant.2.clone.freq, bf16[64,128]{1,0:T(8,128)(2,1)} %bitcast.9, bf16[128,8192]{1,0:T(8,128)(2,1)} %hid.1, bf16[1024,1280]{1,0:T(8,128)(2,1)} %bitcast.5), custom_call_target="tpu_custom_call" | custom-call | tf_op jit(solution)/shard_map/project/pallas_call | solution.py:385
  78.3 6.0 %attend.1 = bf16[128,1024]{1,0:T(8,128)(2,1)} custom-call(s32[16]{0:T(128)} %order.3, s32[64,128]{1,0:T(8,128)} %bitcast.8, bf16[1024,128]{1,0:T(8,128)(2,1)} %get-tuple-element.7.q, bf16[64,128,256]{2,1,0:T(8,128)(2,1)} %get-tuple-element.8.kv), custom_call_target="tpu_custom_call" | custom-call | tf_op jit(solution)/shard_map/attend/pallas_call | solution.py:479
  84.3 49.3 %project_out.1 = bf16[2,2,64,1024]{3,2,1,0:T(8,128)(2,1)} custom-call(bf16[2,64,1024]{2,1,0:T(8,128)(2,1)} %bitcast.7, bf16[1024,1024]{1,0:T(8,128)(2,1)} %w.1), custom_call_target="tpu_custom_call" | custom-call | tf_op jit(solution)/shard_map/project_out/pallas_call | solution.py:618
  133.6 1.9 %copy.9 = bf16[256,1024]{1,0:T(8,128)(2,1)} copy(bf16[256,1024]{1,0:T(8,128)(2,1)} %bitcast.6) | data formatting | bytes 1048576

commit v3 on v2

--- a/solution.py
+++ b/solution.py
@@ -56,7 +56,7 @@
 
 def proj_kernel(
     order, freq, gain, hid, w, q_out, kv_all,
-    hloc, wloc, wg, g32, xbuf, own, far, pairs, kv, rope,
+    hloc, wloc, wg, g32, xbuf, own, far, pairs, kv, rope, row_scale,
     kv_stage, kv_inbox, q_stage, q_inbox,
     lsem, zs, zr, ys, yr, fs, fr, ks, kr, qs, qr,
     gzs, gzr, gxs, gxr, gfs, gfr, gss, gsr,
@@ -112,6 +112,19 @@
         x = hloc[:, pl.ds(pl.multiple_of(c * 128, 128), 128)].astype(F32)
         return acc + x * x
 
+    total = lax.fori_loop(0, NZ * FEAT // 128, square, jnp.zeros((ROWS, 128), F32))
+    mean = jnp.sum(total, axis=1, keepdims=True) / (NZ * FEAT)
+    row_scale[...] = jnp.broadcast_to(lax.rsqrt(mean + 1e-05), (ROWS, HEAD))
+    shard_id = b * NZ + u
+    block = shard_id // (BLOCK // ROWS)
+    first = order[block] * BLOCK + lax.rem(shard_id, BLOCK // ROWS) * ROWS
+    position = (lax.broadcasted_iota(jnp.int32, (ROWS, HEAD), 0) + first).astype(F32)
+    angles = position * freq[...]
+    left_half = lax.broadcasted_iota(jnp.int32, (ROWS, HEAD), 1) < HEAD // 2
+    sines = jnp.sin(angles)
+    rope[0] = jnp.cos(angles)
+    rope[1] = jnp.where(left_half, -sines, sines)
+
     def chunk_from(i, source, direction):
         return remote(
             xbuf.at[i, part(source)], xbuf.at[i, part(source)],
@@ -164,8 +177,6 @@
         far[...] = dot32(xbuf[0], wg[...])
         for direction in range(2):
             send_kv(0, direction, direction)
-        for direction in range(2):
-            send_q(0, direction, direction)
 
     def pair_product(j):
         x = xbuf[2 * j - 1 : 2 * j + 1].reshape(2 * ROWS, FEAT)
@@ -176,6 +187,8 @@
             over_z[tick].wait_recv()
             chunk_from(tick, t, 0).start()
             chunk_from(tick, t, 1).start()
+        if tick == 0:
+            own[...] = dot32(hloc[:, feats(u)], wg[...])
         i = tick - 1
         if 0 <= i < QUARTERED:
             chunk_from(i, t_left, 0).wait_recv()
@@ -196,31 +209,20 @@
                     send_kv(1, direction, 1 - direction)
                     send_kv(1, direction, direction)
                 for direction in range(2):
+                    send_q(0, direction, direction)
+                for direction in range(2):
                     send_q(1, direction, 1 - direction)
     for direction in range(2):
         for piece in range(2):
             send_kv(2, direction, piece)
-    for direction in range(2):
-        send_q(1, direction, direction)
     over_z[QUARTERED].wait_recv()
     over_z[QUARTERED + 1].wait_recv()
     pair_product(3)
     for direction in range(2):
         for piece in range(2):
             send_kv(3, direction, piece)
-
-    total = lax.fori_loop(0, NZ * FEAT // 128, square, jnp.zeros((ROWS, 128), F32))
-    scale = lax.rsqrt(jnp.sum(total, axis=1, keepdims=True) / (NZ * FEAT) + 1e-05)
-    own[...] = dot32(hloc[:, feats(u)], wg[...])
-    shard_id = b * NZ + u
-    block = shard_id // (BLOCK // ROWS)
-    first = order[block] * BLOCK + lax.rem(shard_id, BLOCK // ROWS) * ROWS
-    position = (lax.broadcasted_iota(jnp.int32, (ROWS, HEAD), 0) + first).astype(F32)
-    angles = position * freq[...]
-    left_half = lax.broadcasted_iota(jnp.int32, (ROWS, HEAD), 1) < HEAD // 2
-    sines = jnp.sin(angles)
-    rope[0] = jnp.cos(angles)
-    rope[1] = jnp.where(left_half, -sines, sines)
+    for direction in range(2):
+        send_q(1, direction, direction)
 
     def rotated(x):
         return x * rope[0] + pltpu.roll(x, HEAD // 2, 1) * rope[1]
@@ -230,7 +232,7 @@
         kv_copy(3, 1, piece).wait_recv()
         x = own[:, PIECE_COLS[piece]]
         x = x + kv_inbox[0, 3, piece].astype(F32)
-        x = (x + kv_inbox[1, 3, piece].astype(F32)) * scale
+        x = (x + kv_inbox[1, 3, piece].astype(F32)) * row_scale[...]
         if piece == 0:
             x = rotated(x)
         kv[:, piece * HEAD : (piece + 1) * HEAD] = x.astype(BF16)
@@ -319,24 +321,24 @@
         q_copy(3, 1, piece).wait_recv()
         cols = PIECE_COLS[2 + piece]
         x = own[:, cols] + q_inbox[0, 3, piece].astype(F32)
-        own[:, cols] = (x + q_inbox[1, 3, piece].astype(F32)) * (scale * QSCALE)
+        own[:, cols] = (x + q_inbox[1, 3, piece].astype(F32)) * (row_scale[:, :1] * QSCALE)
         for h in range(piece * HEADS // 2, (piece + 1) * HEADS // 2):
             x = rotated(own[:, h * HEAD : (h + 1) * HEAD])
             q_out[h * ROWS : (h + 1) * ROWS, :] = x.astype(BF16)
 
     gather_tick(0)
     for direction in range(2):
+        send_q(2, direction, 1 - direction)
+    gather_tick(1)
+    for direction in range(2):
         send_q(2, direction, direction)
-    gather_tick(1)
-    for direction in range(2):
-        send_q(2, direction, 1 - direction)
     gather_tick(2)
     gather_tick(3)
     for direction in range(2):
+        send_q(3, direction, 1 - direction)
+    gather_tick(4)
+    for direction in range(2):
         send_q(3, direction, direction)
-    gather_tick(4)
-    for direction in range(2):
-        send_q(3, direction, 1 - direction)
     gather_tick(5)
     gather_tick(6)
     finish_q(0)
@@ -401,6 +403,7 @@
             pltpu.VMEM((3, 2 * ROWS, COLS), F32),
             pltpu.VMEM((ROWS, 2 * HEAD), BF16),
             pltpu.VMEM((2, ROWS, HEAD), F32),
+            pltpu.VMEM((ROWS, HEAD), F32),
             pltpu.VMEM((2, 4, 2, ROWS, HEAD), BF16),
             pltpu.VMEM((2, 4, 2, ROWS, HEAD), BF16),
             pltpu.VMEM((2, 4, 2, ROWS, KCOL // 2), BF16),

time: 136 us -> 135 us (level)
  the two profiles are of different devices: /device:TPU:2 before, /device:TPU:8 now
where the time goes in v3:
time: 135 us
  Pallas kernels  133 us (99%)
  local copies, waits for them, and re-layouts  1.87 us (1%)
    pallas_call x1, Pallas kernels, project(): pl.pallas_call(proj_kernel, out_shape=(jax.ShapeDtypeStruct((HEADS * ROWS...  78.2 us
    pallas_call x1, Pallas kernels, project_out(): pl.pallas_call(out_kernel, out_shape=jax.ShapeDtypeStruct((2, PIECES, PRO...  45.3 us
    pallas_call x1, Pallas kernels, attend(): pl.pallas_call(attend_kernel, out_shape=jax.ShapeDtypeStruct((ROWS, HEADS...  9.54 us

profile of v3, /device:TPU:8, one launch (start us, length us, event | category | flops | bytes accessed | tf_op | source)
XLA Modules:
  0.0 135.0 jit_solution(5718188153555813959)
XLA Ops:
  0.0 78.2 %project.1 = (bf16[1024,128]{1,0:T(8,128)(2,1)}, bf16[64,128,256]{2,1,0:T(8,128)(2,1)}) custom-call(s32[16]{0:T(128)} %order.3, f32[1,128]{1,0:T(1,128)} %constant.2.clone.freq, bf16[64,128]{1,0:T(8,128)(2,1)} %bitcast.9, bf16[128,8192]{1,0:T(8,128)(2,1)} %hid.1, bf16[1024,1280]{1,0:T(8,128)(2,1)} %bitcast.5), custom_call_target="tpu_custom_call" | custom-call | tf_op jit(solution)/shard_map/project/pallas_call | solution.py:387
  78.2 9.5 %attend.1 = bf16[128,1024]{1,0:T(8,128)(2,1)} custom-call(s32[16]{0:T(128)} %order.3, s32[64,128]{1,0:T(8,128)} %bitcast.8, bf16[1024,128]{1,0:T(8,128)(2,1)} %get-tuple-element.7.q, bf16[64,128,256]{2,1,0:T(8,128)(2,1)} %get-tuple-element.8.kv), custom_call_target="tpu_custom_call" | custom-call | tf_op jit(solution)/shard_map/attend/pallas_call | solution.py:482
  87.8 45.3 %project_out.1 = bf16[2,2,64,1024]{3,2,1,0:T(8,128)(2,1)} custom-call(bf16[2,64,1024]{2,1,0:T(8,128)(2,1)} %bitcast.7, bf16[1024,1024]{1,0:T(8,128)(2,1)} %w.1), custom_call_target="tpu_custom_call" | custom-call | tf_op jit(solution)/shard_map/project_out/pallas_call | solution.py:621
  133.1 1.9 %copy.9 = bf16[256,1024]{1,0:T(8,128)(2,1)} copy(bf16[256,1024]{1,0:T(8,128)(2,1)} %bitcast.6) | data formatting | bytes 1048576

commit v4 on v3

--- a/solution.py
+++ b/solution.py
@@ -182,19 +182,19 @@
         x = xbuf[2 * j - 1 : 2 * j + 1].reshape(2 * ROWS, FEAT)
         pairs[j - 1] = dot32(x, wg[...])
 
-    for tick in range(QUARTERED + 2):
+    for tick in range(QUARTERED + 4):
         if tick < QUARTERED:
             over_z[tick].wait_recv()
             chunk_from(tick, t, 0).start()
             chunk_from(tick, t, 1).start()
         if tick == 0:
             own[...] = dot32(hloc[:, feats(u)], wg[...])
-        i = tick - 1
+        i = tick - 2
         if 0 <= i < QUARTERED:
             chunk_from(i, t_left, 0).wait_recv()
             chunk_from(i, t_right, 1).wait_recv()
             pass_on(i).start()
-        i = tick - 2
+        i = tick - 4
         if 0 <= i < QUARTERED:
             remote(
                 xbuf.at[i, part(across)], xbuf.at[i, part(across)], fs.at[i], fr.at[i],
@@ -302,14 +302,14 @@
             x_send(i, 0).start()
             x_send(i, 1).start()
             side(i, 0).start()
-        i = tick - 1
+        i = tick - 2
         if 0 <= i < NZ:
             x_wait(i, 0).wait_recv()
             x_wait(i, 1).wait_recv()
             x_pass(i).start()
             side(i, 1).start()
             side(i, 2).start()
-        i = tick - 2
+        i = tick - 4
         if 0 <= i < NZ:
             remote(
                 shard(b_across, i), shard(b_across, i), gfs.at[i], gfr.at[i], {"blk": b_right}
@@ -330,22 +330,24 @@
     for direction in range(2):
         send_q(2, direction, 1 - direction)
     gather_tick(1)
+    gather_tick(2)
     for direction in range(2):
         send_q(2, direction, direction)
-    gather_tick(2)
     gather_tick(3)
+    gather_tick(4)
     for direction in range(2):
         send_q(3, direction, 1 - direction)
-    gather_tick(4)
-    for direction in range(2):
-        send_q(3, direction, direction)
     gather_tick(5)
     gather_tick(6)
+    for direction in range(2):
+        send_q(3, direction, direction)
+    gather_tick(7)
+    gather_tick(8)
     finish_q(0)
-    gather_tick(7)
+    gather_tick(9)
     finish_q(1)
-    gather_tick(8)
-    gather_tick(9)
+    gather_tick(10)
+    gather_tick(11)
     place_own.wait()
     for i in range(NZ):
         for m in range(4):

time: 135 us -> 131 us (0.970)
  Pallas kernels: 133 us -> 129 us
    pallas_call x1, Pallas kernels: 45.3 us -> 51 us  [project_out(): pl.pallas_call(out_kernel, out_shape=jax.ShapeDtypeStruct((2, PIECES, PRO...]
    pallas_call x1, Pallas kernels: 78.2 us -> 72.6 us  [project(): pl.pallas_call(proj_kernel, out_shape=(jax.ShapeDtypeStruct((HEADS * ROWS...]
    pallas_call x1, Pallas kernels: 9.54 us -> 5.04 us  [attend(): pl.pallas_call(attend_kernel, out_shape=jax.ShapeDtypeStruct((ROWS, HEADS...]
where the time goes in v4:
time: 131 us
  Pallas kernels  129 us (98%)
  local copies, waits for them, and re-layouts  1.87 us (1%)
    pallas_call x1, Pallas kernels, project(): pl.pallas_call(proj_kernel, out_shape=(jax.ShapeDtypeStruct((HEADS * ROWS...  72.6 us
    pallas_call x1, Pallas kernels, project_out(): pl.pallas_call(out_kernel, out_shape=jax.ShapeDtypeStruct((2, PIECES, PRO...  51 us
    pallas_call x1, Pallas kernels, attend(): pl.pallas_call(attend_kernel, out_shape=jax.ShapeDtypeStruct((ROWS, HEADS...  5.04 us

profile of v4, /device:TPU:8, one launch (start us, length us, event | category | flops | bytes accessed | tf_op | source)
XLA Modules:
  0.0 130.6 jit_solution(6917230062934342530)
XLA Ops:
  0.0 72.6 %project.1 = (bf16[1024,128]{1,0:T(8,128)(2,1)}, bf16[64,128,256]{2,1,0:T(8,128)(2,1)}) custom-call(s32[16]{0:T(128)} %order.3, f32[1,128]{1,0:T(1,128)} %constant.2.clone.freq, bf16[64,128]{1,0:T(8,128)(2,1)} %bitcast.9, bf16[128,8192]{1,0:T(8,128)(2,1)} %hid.1, bf16[1024,1280]{1,0:T(8,128)(2,1)} %bitcast.5), custom_call_target="tpu_custom_call" | custom-call | tf_op jit(solution)/shard_map/project/pallas_call | solution.py:389
  72.6 5.0 %attend.1 = bf16[128,1024]{1,0:T(8,128)(2,1)} custom-call(s32[16]{0:T(128)} %order.3, s32[64,128]{1,0:T(8,128)} %bitcast.8, bf16[1024,128]{1,0:T(8,128)(2,1)} %get-tuple-element.7.q, bf16[64,128,256]{2,1,0:T(8,128)(2,1)} %get-tuple-element.8.kv), custom_call_target="tpu_custom_call" | custom-call | tf_op jit(solution)/shard_map/attend/pallas_call | solution.py:484
  77.7 51.0 %project_out.1 = bf16[2,2,64,1024]{3,2,1,0:T(8,128)(2,1)} custom-call(bf16[2,64,1024]{2,1,0:T(8,128)(2,1)} %bitcast.7, bf16[1024,1024]{1,0:T(8,128)(2,1)} %w.1), custom_call_target="tpu_custom_call" | custom-call | tf_op jit(solution)/shard_map/project_out/pallas_call | solution.py:623
  128.7 1.9 %copy.9 = bf16[256,1024]{1,0:T(8,128)(2,1)} copy(bf16[256,1024]{1,0:T(8,128)(2,1)} %bitcast.6) | data formatting | bytes 1048576

commit v5 on v4

--- a/solution.py
+++ b/solution.py
@@ -497,7 +497,8 @@
     )(order, docs, q, kv)
 
 
-PIECES = 2
+PIECES = 4
+HOPS = 4
 PROWS = ROWS // PIECES
 OUTW = 1024
 
@@ -569,46 +570,51 @@
             {"tp": t_right if direction == 0 else t_left},
         )
 
-    for p in range(PIECES):
-        z_step(p, 0)
-    load_w.wait()
-    for copy in own_copies:
-        copy.wait()
-    for h in range(1, 5):
-        z_step(0, h)
-    for p in range(PIECES):
-        more = p + 1 < PIECES
-        value = product(p, 2)
-        for side in range(2):
-            far_stage[p, side] = value[:, half(side)].astype(BF16)
-            far_send(p, side).start()
-        if more:
-            z_step(p + 1, 1)
-        right = product(p, 1)
-        near_stage[p, 0, 1] = right[:, half(1)].astype(BF16)
-        near_send(p, 0, 1).start()
-        left = product(p, 3)
-        near_stage[p, 1, 0] = left[:, half(0)].astype(BF16)
-        near_send(p, 1, 0).start()
-        if more:
-            z_step(p + 1, 2)
-        far_send(p, 0).wait_recv()
-        near_stage[p, 0, 0] = (right[:, half(0)] + far_box[p, 0].astype(F32)).astype(BF16)
-        near_send(p, 0, 0).start()
-        far_send(p, 1).wait_recv()
-        near_stage[p, 1, 1] = (left[:, half(1)] + far_box[p, 1].astype(F32)).astype(BF16)
-        near_send(p, 1, 1).start()
-        if more:
-            z_step(p + 1, 3)
-        mine = product(p, 0)
-        if more:
-            z_step(p + 1, 4)
+    def finish(p):
+        mine = sides[p]
         for side in range(2):
             near_send(p, 0, side).wait_recv()
             near_send(p, 1, side).wait_recv()
             summed = mine[:, half(side)] + near_box[p, 0, side].astype(F32)
             summed = summed + near_box[p, 1, side].astype(F32)
             out[:, p, :, half(side)] = summed.reshape(2, PROWS, OUTW // 2).astype(BF16)
+
+    z_step(0, 0)
+    load_w.wait()
+    for copy in own_copies:
+        copy.wait()
+    sides = {}
+    for slot in range(1, PIECES + HOPS + 2):
+        for p in range(PIECES):
+            if 0 <= slot - p <= HOPS:
+                z_step(p, slot - p)
+        p = slot - HOPS
+        if 0 <= p < PIECES:
+            value = product(p, 2)
+            for side in range(2):
+                far_stage[p, side] = value[:, half(side)].astype(BF16)
+                far_send(p, side).start()
+            right = product(p, 1)
+            near_stage[p, 0, 1] = right[:, half(1)].astype(BF16)
+            near_send(p, 0, 1).start()
+            left = product(p, 3)
+            near_stage[p, 1, 0] = left[:, half(0)].astype(BF16)
+            near_send(p, 1, 0).start()
+            sides[p] = right[:, half(0)], left[:, half(1)]
+        p = slot - HOPS - 1
+        if 0 <= p < PIECES:
+            right, left = sides[p]
+            far_send(p, 0).wait_recv()
+            near_stage[p, 0, 0] = (right + far_box[p, 0].astype(F32)).astype(BF16)
+            near_send(p, 0, 0).start()
+            far_send(p, 1).wait_recv()
+            near_stage[p, 1, 1] = (left + far_box[p, 1].astype(F32)).astype(BF16)
+            near_send(p, 1, 1).start()
+            mine = product(p, 0)
+            sides[p] = mine
+        p = slot - HOPS - 2
+        if 0 <= p < PIECES:
+            finish(p)
     for p in range(PIECES):
         for direction in range(2):
             for h in range(z_hops(p, direction)):

time: 131 us -> 127 us (0.969)
  Pallas kernels: 129 us -> 125 us
    pallas_call x1, Pallas kernels: 51 us -> 44.8 us  [project_out(): pl.pallas_call(out_kernel, out_shape=jax.ShapeDtypeStruct((2, PIECES, PRO...]
    pallas_call x1, Pallas kernels: 5.04 us -> 7.04 us  [attend(): pl.pallas_call(attend_kernel, out_shape=jax.ShapeDtypeStruct((ROWS, HEADS...]
where the time goes in v5:
time: 127 us; the launch traced here: 126 us
  Pallas kernels  125 us (98%)
  local copies, waits for them, and re-layouts  1.87 us (1%)
    pallas_call x1, Pallas kernels, project(): pl.pallas_call(proj_kernel, out_shape=(jax.ShapeDtypeStruct((HEADS * ROWS...  72.6 us
    pallas_call x1, Pallas kernels, project_out(): pl.pallas_call(out_kernel, out_shape=jax.ShapeDtypeStruct((2, PIECES, PRO...  44.8 us
    pallas_call x1, Pallas kernels, attend(): pl.pallas_call(attend_kernel, out_shape=jax.ShapeDtypeStruct((ROWS, HEADS...  7.04 us

profile of v5, /device:TPU:8, one launch (start us, length us, event | category | flops | bytes accessed | tf_op | source)
XLA Modules:
  0.0 126.4 jit_solution(7168076462440443975)
XLA Ops:
  0.0 72.6 %project.1 = (bf16[1024,128]{1,0:T(8,128)(2,1)}, bf16[64,128,256]{2,1,0:T(8,128)(2,1)}) custom-call(s32[16]{0:T(128)} %order.3, f32[1,128]{1,0:T(1,128)} %constant.2.clone.freq, bf16[64,128]{1,0:T(8,128)(2,1)} %bitcast.9, bf16[128,8192]{1,0:T(8,128)(2,1)} %hid.1, bf16[1024,1280]{1,0:T(8,128)(2,1)} %bitcast.5), custom_call_target="tpu_custom_call" | custom-call | tf_op jit(solution)/shard_map/project/pallas_call | solution.py:389
  72.6 7.0 %attend.1 = bf16[128,1024]{1,0:T(8,128)(2,1)} custom-call(s32[16]{0:T(128)} %order.3, s32[64,128]{1,0:T(8,128)} %bitcast.8, bf16[1024,128]{1,0:T(8,128)(2,1)} %get-tuple-element.7.q, bf16[64,128,256]{2,1,0:T(8,128)(2,1)} %get-tuple-element.8.kv), custom_call_target="tpu_custom_call" | custom-call | tf_op jit(solution)/shard_map/attend/pallas_call | solution.py:484
  79.7 44.8 %project_out.1 = bf16[2,4,32,1024]{3,2,1,0:T(8,128)(2,1)} custom-call(bf16[4,32,1024]{2,1,0:T(8,128)(2,1)} %bitcast.7, bf16[1024,1024]{1,0:T(8,128)(2,1)} %w.1), custom_call_target="tpu_custom_call" | custom-call | tf_op jit(solution)/shard_map/project_out/pallas_call | solution.py:629
  124.5 1.9 %copy.9 = bf16[256,1024]{1,0:T(8,128)(2,1)} copy(bf16[256,1024]{1,0:T(8,128)(2,1)} %bitcast.6) | data formatting | bytes 1048576

commit v6 on v5

--- a/solution.py
+++ b/solution.py
@@ -449,30 +449,37 @@
     causal = row <= lane
     starts = jnp.broadcast_to(starts, (128, ROWS))
 
-    def step(i, carry):
+    def place(k_block):
+        k_block = jnp.maximum(k_block, 0)
+        return inverse[k_block // per] * per + lax.rem(k_block, per)
+
+    def scores_of(i):
         k_block = q_block - i
-        at = inverse[k_block // per] * per + lax.rem(k_block, per)
-        k = kv[at, :, :HEAD]
-        v = kv[at, :, HEAD:]
         scores = lax.dot_general(
-            k, q[...], (((1,), (1,)), ((), ())), preferred_element_type=F32
+            kv[place(k_block), :, :HEAD], q[...], (((1,), (1,)), ((), ())), preferred_element_type=F32
         )
         allowed = (row + k_block * 128 >= starts) & (causal | (i > 0))
         bias = jnp.where(allowed, 0.0, NEG_BIG)
-        scores = scores + jnp.concatenate([bias] * HEADS, axis=1)
+        return scores + jnp.concatenate([bias] * HEADS, axis=1)
+
+    def mix(i, weights):
+        return lax.dot_general(
+            kv[place(q_block - i), :, HEAD:], weights.astype(BF16), (((0,), (0,)), ((), ())),
+            preferred_element_type=F32,
+        )
+
+    def step(j, carry):
+        near, past = scores_of(2 * j), scores_of(2 * j + 1)
         m_old = m_ref[...]
-        m_new = jnp.maximum(m_old, jnp.max(scores, axis=0, keepdims=True))
-        weights = jnp.exp2(scores - m_new)
+        m_new = jnp.maximum(m_old, jnp.max(jnp.maximum(near, past), axis=0, keepdims=True))
+        near, past = jnp.exp2(near - m_new), jnp.exp2(past - m_new)
         factor = jnp.exp2(m_old - m_new)
         m_ref[...] = m_new
-        l_ref[...] = l_ref[...] * factor + jnp.sum(weights, axis=0, keepdims=True)
-        mixed = lax.dot_general(
-            v, weights.astype(BF16), (((0,), (0,)), ((), ())), preferred_element_type=F32
-        )
-        acc[...] = acc[...] * factor + mixed
+        l_ref[...] = l_ref[...] * factor + jnp.sum(near + past, axis=0, keepdims=True)
+        acc[...] = acc[...] * factor + (mix(2 * j, near) + mix(2 * j + 1, past))
         return carry
 
-    lax.fori_loop(0, count, step, 0)
+    lax.fori_loop(0, (count + 1) // 2, step, 0)
     result = acc[...] / l_ref[...]
     for h in range(HEADS):
         part = result[:, h * ROWS : (h + 1) * ROWS]

time: 127 us -> 127 us (level)
  the two profiles are of different devices: /device:TPU:8 before, /device:TPU:4 now
where the time goes in v6:
time: 127 us
  Pallas kernels  125 us (98%)
  local copies, waits for them, and re-layouts  1.87 us (1%)
    pallas_call x1, Pallas kernels, project(): pl.pallas_call(proj_kernel, out_shape=(jax.ShapeDtypeStruct((HEADS * ROWS...  73.2 us
    pallas_call x1, Pallas kernels, project_out(): pl.pallas_call(out_kernel, out_shape=jax.ShapeDtypeStruct((2, PIECES, PRO...  41.2 us
    pallas_call x1, Pallas kernels, attend(): pl.pallas_call(attend_kernel, out_shape=jax.ShapeDtypeStruct((ROWS, HEADS...  10.5 us

profile of v6, /device:TPU:4, one launch (start us, length us, event | category | flops | bytes accessed | tf_op | source)
XLA Modules:
  0.0 126.8 jit_solution(3854108806143239079)
XLA Ops:
  0.0 73.2 %project.1 = (bf16[1024,128]{1,0:T(8,128)(2,1)}, bf16[64,128,256]{2,1,0:T(8,128)(2,1)}) custom-call(s32[16]{0:T(128)} %order.3, f32[1,128]{1,0:T(1,128)} %constant.2.clone.freq, bf16[64,128]{1,0:T(8,128)(2,1)} %bitcast.9, bf16[128,8192]{1,0:T(8,128)(2,1)} %hid.1, bf16[1024,1280]{1,0:T(8,128)(2,1)} %bitcast.5), custom_call_target="tpu_custom_call" | custom-call | tf_op jit(solution)/shard_map/project/pallas_call | solution.py:389
  73.2 10.5 %attend.1 = bf16[128,1024]{1,0:T(8,128)(2,1)} custom-call(s32[16]{0:T(128)} %order.3, s32[64,128]{1,0:T(8,128)} %bitcast.8, bf16[1024,128]{1,0:T(8,128)(2,1)} %get-tuple-element.7.q, bf16[64,128,256]{2,1,0:T(8,128)(2,1)} %get-tuple-element.8.kv), custom_call_target="tpu_custom_call" | custom-call | tf_op jit(solution)/shard_map/attend/pallas_call | solution.py:491
  83.8 41.2 %project_out.1 = bf16[2,4,32,1024]{3,2,1,0:T(8,128)(2,1)} custom-call(bf16[4,32,1024]{2,1,0:T(8,128)(2,1)} %bitcast.7, bf16[1024,1024]{1,0:T(8,128)(2,1)} %w.1), custom_call_target="tpu_custom_call" | custom-call | tf_op jit(solution)/shard_map/project_out/pallas_call | solution.py:636
  125.0 1.9 %copy.9 = bf16[256,1024]{1,0:T(8,128)(2,1)} copy(bf16[256,1024]{1,0:T(8,128)(2,1)} %bitcast.6) | data formatting | bytes 1048576

commit v7 on v6

--- a/solution.py
+++ b/solution.py
@@ -393,7 +393,7 @@
             jax.ShapeDtypeStruct((8 * NZ, ROWS, 2 * HEAD), BF16),
         ),
         in_specs=[SM, VM, VM, HBM, HBM],
-        out_specs=(VM, VM),
+        out_specs=(VM, HBM),
         scratch_shapes=[
             pltpu.VMEM((ROWS, NZ * FEAT), BF16),
             pltpu.VMEM((FEAT, COLS), BF16),

time: 127 us -> 127 us (level)
  the two profiles are of different devices: /device:TPU:4 before, /device:TPU:8 now
where the time goes in v7:
time: 127 us; the launch traced here: 124 us
  Pallas kernels  123 us (97%)
  local copies, waits for them, and re-layouts  1.87 us (1%)
    pallas_call x1, Pallas kernels, project(): pl.pallas_call(proj_kernel, out_shape=(jax.ShapeDtypeStruct((HEADS * ROWS...  72.3 us
    pallas_call x1, Pallas kernels, project_out(): pl.pallas_call(out_kernel, out_shape=jax.ShapeDtypeStruct((2, PIECES, PRO...  45.8 us
    pallas_call x1, Pallas kernels, attend(): pl.pallas_call(attend_kernel, out_shape=jax.ShapeDtypeStruct((ROWS, HEADS...  4.48 us

profile of v7, /device:TPU:8, one launch (start us, length us, event | category | flops | bytes accessed | tf_op | source)
XLA Modules:
  0.0 124.5 jit_solution(5085620056933075767)
XLA Ops:
  0.0 72.3 %project.1 = (bf16[1024,128]{1,0:T(8,128)(2,1)}, bf16[64,128,256]{2,1,0:T(8,128)(2,1)}) custom-call(s32[16]{0:T(128)} %order.3, f32[1,128]{1,0:T(1,128)} %constant.2.clone.freq, bf16[64,128]{1,0:T(8,128)(2,1)} %bitcast.9, bf16[128,8192]{1,0:T(8,128)(2,1)} %hid.1, bf16[1024,1280]{1,0:T(8,128)(2,1)} %bitcast.5), custom_call_target="tpu_custom_call" | custom-call | tf_op jit(solution)/shard_map/project/pallas_call | solution.py:389
  72.3 4.5 %attend.1 = bf16[128,1024]{1,0:T(8,128)(2,1)} custom-call(s32[16]{0:T(128)} %order.3, s32[64,128]{1,0:T(8,128)} %bitcast.8, bf16[1024,128]{1,0:T(8,128)(2,1)} %get-tuple-element.7.q, bf16[64,128,256]{2,1,0:T(8,128)(2,1)} %get-tuple-element.8.kv), custom_call_target="tpu_custom_call" | custom-call | tf_op jit(solution)/shard_map/attend/pallas_call | solution.py:491
  76.8 45.8 %project_out.1 = bf16[2,4,32,1024]{3,2,1,0:T(8,128)(2,1)} custom-call(bf16[4,32,1024]{2,1,0:T(8,128)(2,1)} %bitcast.7, bf16[1024,1024]{1,0:T(8,128)(2,1)} %w.1), custom_call_target="tpu_custom_call" | custom-call | tf_op jit(solution)/shard_map/project_out/pallas_call | solution.py:636
  122.6 1.9 %copy.9 = bf16[256,1024]{1,0:T(8,128)(2,1)} copy(bf16[256,1024]{1,0:T(8,128)(2,1)} %bitcast.6) | data formatting | bytes 1048576
